TPU v7x, 512 devices: a whole 4x8x8 slice. The times are simulated.
512 devices in a mesh: elem: 64 (over x, y_lo, z), band: 8 (over y_hi, core).
Axes of the slice: x: 4, y: 8 (y_hi: 4, y_lo: 2; y = y_hi * 2 + y_lo), z: 8, core: 2. Of those that a mesh axis runs over, the one named last changes fastest.
Arguments:
- start_bands: bfloat16 [384, 256, 1024], P('elem', None, 'band'), may hold values from -6 to 6
- blocks: bfloat16 [384, 5, 256, 256], P('elem'), may hold values from -0.125 to 0.125
- neighbours: int32 [384, 5], P('elem'), may hold values from 0 to 383, as said below
- band_order: int32 [1024], replicated, may hold values from 0 to 1023, each once
- rotation: bfloat16 [1024, 1024], P('elem', 'band'), may hold values from -0.1875 to 0.1875
Outputs:
- final_bands: bfloat16 [384, 256, 1024], P('elem', None, 'band')
Inputs may be any that keep to these rules, and one draw needn't show every extreme that they name: `neighbours`: the elements form a periodic grid of 128 columns of 3 elements; column c holds the ids c * 3 to c * 3 + 2 in a drawn order. Row e lists e, the element at the same place in the previous column, the one in the next column, then the previous and the next element within e's column, periodically, in that order. `band_order`: A permutation of the band numbers.
All inputs are finite; a program needn't handle non-finite values.
Results may differ from a plain program's by a relative error of at most 0.01.
Values may be sent and summed in bfloat16 or wider, within the bound.
A program may use at most 64 MiB of HBM per device.

v0:
```python
import jax
import jax.numpy as jnp
from jax import lax
from jax.sharding import PartitionSpec as P

GY = 3


def extended_2(cells, sides, width):
    for axis, dim in sides:
        count = lax.axis_size(axis)
        head = lax.slice_in_dim(cells, 0, width, axis=dim)
        tail = lax.slice_in_dim(cells, cells.shape[dim] - width, cells.shape[dim], axis=dim)
        cells = jnp.concatenate(
            [
                lax.ppermute(tail, axis, [(i, (i + 1) % count) for i in range(count)]),
                cells,
                lax.ppermute(head, axis, [((i + 1) % count, i) for i in range(count)]),
            ],
            axis=dim,
        )
    return cells


def apply_blocks(current, blocks, local_links):
    extended = extended_2(current, (("elem", 0),), GY)
    picked = jnp.take(extended, local_links, axis=0)
    return jnp.einsum("esij,esjm->eim", blocks, picked, preferred_element_type=jnp.float32)


def chebyshev(initial, blocks, local_links):
    first_term = apply_blocks(initial, blocks, local_links).astype(jnp.bfloat16)
    second_term = (
        2.0 * apply_blocks(first_term, blocks, local_links) - initial.astype(jnp.float32)
    ).astype(jnp.bfloat16)
    third_term = (
        2.0 * apply_blocks(second_term, blocks, local_links) - first_term.astype(jnp.float32)
    ).astype(jnp.bfloat16)
    return third_term


def body(start_bands, blocks, neighbours, band_order, rotation):
    elem_count = start_bands.shape[0]
    basis = start_bands.shape[1]
    width = start_bands.shape[2]
    everything = elem_count * lax.axis_size("elem")
    first_id = lax.axis_index("elem") * elem_count
    local_links = jnp.mod(neighbours - first_id + GY, everything)
    filtered = chebyshev(start_bands, blocks, local_links)
    rotation_cols = lax.all_gather(rotation, "elem", axis=0, tiled=True)
    rotation_full = lax.all_gather(rotation_cols, "band", axis=1, tiled=True)
    permuted_full = jnp.zeros_like(rotation_full).at[band_order].set(rotation_full)
    flat_rows = filtered.reshape(elem_count * basis, width)
    band_rows = lax.all_to_all(flat_rows, "band", split_axis=0, concat_axis=1, tiled=True)
    mixed_rows = jnp.dot(band_rows, permuted_full, preferred_element_type=jnp.float32).astype(
        jnp.bfloat16
    )
    returned = lax.all_to_all(mixed_rows, "band", split_axis=1, concat_axis=0, tiled=True)
    rotated = returned.reshape(elem_count, basis, width)
    return chebyshev(rotated, blocks, local_links)


def solution(mesh):
    return jax.shard_map(
        body,
        mesh=mesh,
        in_specs=(
            P("elem", None, "band"),
            P("elem", None, None, None),
            P("elem", None),
            P(),
            P("elem", "band"),
        ),
        out_specs=P("elem", None, "band"),
        check_vma=False,
    )
```

profile of v0, /device:TPU:1, one launch (start us, length us, event | category | flops | bytes accessed | tf_op | source)
XLA Modules:
  0.0 339.2 jit_solution(324917954390206005)
XLA Ops:
  6.5 0.0 all-gather.2.cloned.1.call-start
  6.5 1.0 fusion.118
  7.6 4.8 %collective-permute-start = (bf16[3,256,128]{2,1,0:T(8,128)(2,1)S(1)}, bf16[3,256,128]{2,1,0:T(8,128)(2,1)S(1)}, u32[]{:S(2)}, u32[]{:S(2)}) collective-permute-start(bf16[3,256,128]{2,1,0:T(8,128)(2,1)S(1)} %get-tuple-element.18), channel_id=1, source_target_pairs={{0,8},{8,16},{16,24},{24,32},{32,40},{40,48},{48,56},{56,64},{64,7... | collective-permute-start | bytes 589832 | tf_op jit(solution)/shard_map/ppermute | solution.py:16
  12.4 11.8 %collective-permute-start.1 = (bf16[3,256,128]{2,1,0:T(8,128)(2,1)S(1)}, bf16[3,256,128]{2,1,0:T(8,128)(2,1)S(1)}, u32[]{:S(2)}, u32[]{:S(2)}) collective-permute-start(bf16[3,256,128]{2,1,0:T(8,128)(2,1)S(1)} %get-tuple-element.19), channel_id=1, source_target_pairs={{8,0},{16,8},{24,16},{32,24},{40,32},{48,40},{56,48},{64,56},{72,6... | collective-permute-start | bytes 589832 | tf_op jit(solution)/shard_map/ppermute | solution.py:18
  24.2 136.4 %all_gather.6 = bf16[1024,128]{1,0:T(8,128)(2,1)} all-gather(bf16[16,128]{1,0:T(8,128)(2,1)} %param.11), channel_id=1, replica_groups=mesh['elem'=64,'band'=8] {'elem'}, dimensions={0}, use_global_device_ids=true | all-gather | bytes 266240 | tf_op jit(solution)/shard_map/all_gather | solution.py:50
  160.6 0.0 all-gather.2.cloned.1.call-update
  160.6 0.7 compare_and_fusion
  161.3 0.1 reshape.89
  161.4 0.0 collective-permute-done
  161.4 0.0 collective-permute-done.1
  161.5 1.1 pad_maximum_fusion
  162.5 0.9 gather_fusion
  163.5 2.3 copy.9
  165.8 4.2 %fusion.91 = bf16[6,256,128]{1,2,0:T(8,128)(2,1)S(1)} fusion(bf16[6,5,256,256]{3,2,1,0:T(8,128)(2,1)} %param.8, bf16[6,5,256,128]{2,3,1,0:T(8,128)(2,1)} %copy.9, pred[6,5]{1,0:T(8,128)(4,1)S(1)} %get-tuple-element.6), kind=kOutput, calls=%fused_computation.51 | convolution fusion | flops 504496128 | bytes 6291486 | tf_op jit(solution)/shard_map/esij,esjm->eim/dot_general | solution.py:28
  170.0 1.9 collective-permute-start.2
  171.9 7.6 %collective-permute-start.3 = (bf16[3,256,128]{1,2,0:T(8,128)(2,1)S(1)}, bf16[3,256,128]{1,2,0:T(8,128)(2,1)S(1)}, u32[]{:S(2)}, u32[]{:S(2)}) collective-permute-start(bf16[3,256,128]{1,2,0:T(8,128)(2,1)S(1)} %get-tuple-element.17), channel_id=1, source_target_pairs={{8,0},{16,8},{24,16},{32,24},{40,32},{48,40},{56,48},{64,56},{72,6... | collective-permute-start | bytes 589832 | tf_op jit(solution)/shard_map/ppermute | solution.py:18
  179.5 0.0 copy-done
  179.5 0.2 copy.10
  179.7 0.9 collective-permute-done.2
  180.6 1.5 collective-permute-done.3
  182.1 0.1 pad_maximum_fusion.1
  182.2 0.7 gather_fusion.1
  182.9 3.5 %fusion.81 = bf16[6,256,128]{1,2,0:T(8,128)(2,1)S(1)} fusion(bf16[6,5,256,256]{3,2,1,0:T(8,128)(2,1)} %param.8, bf16[6,5,256,128]{2,3,1,0:T(8,128)(2,1)S(1)} %bitcast.124, pred[6,5]{1,0:T(8,128)(4,1)S(1)} %get-tuple-element.6, bf16[6,256,128]{1,2,0:T(8,128)(2,1)S(1)} %copy.10), kind=kOutput, calls=%fused_computation.46 | convolution fusion | flops 505085952 | bytes 6684702 | tf_op jit(solution)/shard_map/esij,esjm->eim/dot_general | solution.py:28
  186.4 1.9 collective-permute-start.4
  188.4 8.0 %collective-permute-start.5 = (bf16[3,256,128]{1,2,0:T(8,128)(2,1)S(1)}, bf16[3,256,128]{1,2,0:T(8,128)(2,1)S(1)}, u32[]{:S(2)}, u32[]{:S(2)}) collective-permute-start(bf16[3,256,128]{1,2,0:T(8,128)(2,1)S(1)} %get-tuple-element.15), channel_id=1, source_target_pairs={{8,0},{16,8},{24,16},{32,24},{40,32},{48,40},{56,48},{64,56},{72,6... | collective-permute-start | bytes 589832 | tf_op jit(solution)/shard_map/ppermute | solution.py:18
  196.4 1.1 collective-permute-done.4
  197.5 6.8 %collective-permute-done.5 = bf16[3,256,128]{1,2,0:T(8,128)(2,1)S(1)} collective-permute-done((bf16[3,256,128]{1,2,0:T(8,128)(2,1)S(1)}, bf16[3,256,128]{1,2,0:T(8,128)(2,1)S(1)}, u32[]{:S(2)}, u32[]{:S(2)}) %collective-permute-start.5) | collective-permute-done | bytes 196640 | tf_op jit(solution)/shard_map/ppermute | solution.py:18
  204.3 0.1 pad_maximum_fusion.2
  204.4 0.7 gather_fusion.2
  205.1 0.0 copy-start.1
  205.1 3.5 %fusion.78 = bf16[6,256,128]{1,2,0:T(8,128)(2,1)S(1)} fusion(bf16[6,5,256,256]{3,2,1,0:T(8,128)(2,1)} %param.8, bf16[6,5,256,128]{2,3,1,0:T(8,128)(2,1)S(1)} %bitcast.125, pred[6,5]{1,0:T(8,128)(4,1)S(1)} %get-tuple-element.6, bf16[6,256,128]{1,2,0:T(8,128)(2,1)S(1)} %fusion.91), kind=kOutput, calls=%fused_computation.45 | convolution fusion | flops 505085952 | bytes 6684702 | tf_op jit(solution)/shard_map/esij,esjm->eim/dot_general | solution.py:28
  208.6 0.9 copy.11
  209.6 38.3 %all-to-all-start = ((bf16[8,192,128]{2,1,0:T(8,128)(2,1)}), bf16[8,192,128]{2,1,0:T(8,128)(2,1)S(1)}, u32[]{:S(2)}, u32[]{:S(2)}) async-start(bf16[8,192,128]{2,1,0:T(8,128)(2,1)} %bitcast.12), calls=%async_computation | async-start | bytes 786432 | tf_op jit(solution)/shard_map/all_to_all | solution.py:54
  247.9 0.0 copy-done.1
  247.9 0.0 all-gather.2.cloned.1.call-done
  247.9 6.6 %scatter_custom_fusion = bf16[1024,1024]{1,0:T(8,128)(2,1)S(1)} fusion(s32[1024]{0:T(1024)S(1)} %compare_select_fusion.1, bf16[1024,1024]{1,0:T(8,128)(2,1)} %all-gather.2.cloned.1.call-done, bf16[]{:T(256)} %constant.37.clone.1), kind=kCustom, calls=%fused_computation.53 | custom fusion | bytes 2097664 | tf_op jit(solution)/shard_map/scatter | solution.py:52
  254.5 5.7 %all-to-all-done = bf16[8,192,128]{2,1,0:T(8,128)(2,1)S(1)} async-done(((bf16[8,192,128]{2,1,0:T(8,128)(2,1)}), bf16[8,192,128]{2,1,0:T(8,128)(2,1)S(1)}, u32[]{:S(2)}, u32[]{:S(2)}) %all-to-all-start) | async-done | bytes 393248 | tf_op jit(solution)/shard_map/all_to_all | solution.py:54
  260.2 0.6 fusion.90
  260.8 0.1 copy.30
  260.9 15.1 %all_to_all.35 = bf16[192,8,128]{2,0,1:T(8,128)(2,1)S(1)} all-to-all(bf16[192,8,128]{2,0,1:T(8,128)(2,1)S(1)} %bitcast.127), channel_id=1, replica_groups=mesh['elem'=64,'band'=8] {'band'}, dimensions={1} | all-to-all | bytes 786432 | tf_op jit(solution)/shard_map/all_to_all | solution.py:58
  276.0 1.9 collective-permute-start.6
  278.0 8.9 %collective-permute-start.7 = (bf16[3,256,128]{2,1,0:T(8,128)(2,1)S(1)}, bf16[3,256,128]{2,1,0:T(8,128)(2,1)S(1)}, u32[]{:S(2)}, u32[]{:S(2)}) collective-permute-start(bf16[3,256,128]{2,1,0:T(8,128)(2,1)S(1)} %bitcast.128), channel_id=1, source_target_pairs={{8,0},{16,8},{24,16},{32,24},{40,32},{48,40},{56,48},{64,56},{72,6... | collective-permute-start | bytes 589832 | tf_op jit(solution)/shard_map/ppermute | solution.py:18
  286.9 2.1 collective-permute-done.6
  289.0 0.9 collective-permute-done.7
  289.9 0.1 pad_maximum_fusion.3
  290.0 0.9 gather_fusion.3
  290.9 2.3 copy.14
  293.2 4.1 %fusion.94 = bf16[6,256,128]{1,2,0:T(8,128)(2,1)S(1)} fusion(bf16[6,5,256,256]{3,2,1,0:T(8,128)(2,1)} %param.8, bf16[6,5,256,128]{2,3,1,0:T(8,128)(2,1)} %copy.14, pred[6,5]{1,0:T(8,128)(4,1)S(1)} %get-tuple-element.6), kind=kOutput, calls=%fused_computation.52 | convolution fusion | flops 504496128 | bytes 6291486 | tf_op jit(solution)/shard_map/esij,esjm->eim/dot_general | solution.py:28
  297.4 1.9 collective-permute-start.8
  299.3 8.5 %collective-permute-start.9 = (bf16[3,256,128]{1,2,0:T(8,128)(2,1)S(1)}, bf16[3,256,128]{1,2,0:T(8,128)(2,1)S(1)}, u32[]{:S(2)}, u32[]{:S(2)}) collective-permute-start(bf16[3,256,128]{1,2,0:T(8,128)(2,1)S(1)} %get-tuple-element.11), channel_id=1, source_target_pairs={{8,0},{16,8},{24,16},{32,24},{40,32},{48,40},{56,48},{64,56},{72,6... | collective-permute-start | bytes 589832 | tf_op jit(solution)/shard_map/ppermute | solution.py:18
  307.8 0.2 copy.15
  308.0 0.7 collective-permute-done.8
  308.8 1.5 collective-permute-done.9
  310.2 0.1 pad_maximum_fusion.4
  310.3 0.7 gather_fusion.4
  311.0 3.5 %fusion.75 = bf16[6,256,128]{1,2,0:T(8,128)(2,1)S(1)} fusion(bf16[6,5,256,256]{3,2,1,0:T(8,128)(2,1)} %param.8, bf16[6,5,256,128]{2,3,1,0:T(8,128)(2,1)S(1)} %bitcast.126, pred[6,5]{1,0:T(8,128)(4,1)S(1)} %get-tuple-element.6, bf16[6,256,128]{1,2,0:T(8,128)(2,1)S(1)} %copy.15), kind=kOutput, calls=%fused_computation.44 | convolution fusion | flops 505085952 | bytes 6684702 | tf_op jit(solution)/shard_map/esij,esjm->eim/dot_general | solution.py:28
  314.6 1.9 collective-permute-start.10
  316.5 8.0 %collective-permute-start.11 = (bf16[3,256,128]{1,2,0:T(8,128)(2,1)S(1)}, bf16[3,256,128]{1,2,0:T(8,128)(2,1)S(1)}, u32[]{:S(2)}, u32[]{:S(2)}) collective-permute-start(bf16[3,256,128]{1,2,0:T(8,128)(2,1)S(1)} %get-tuple-element.9), channel_id=1, source_target_pairs={{8,0},{16,8},{24,16},{32,24},{40,32},{48,40},{56,48},{64,56},{72,6... | collective-permute-start | bytes 589832 | tf_op jit(solution)/shard_map/ppermute | solution.py:18
  324.6 1.1 collective-permute-done.10
  325.7 1.5 collective-permute-done.11
  327.1 0.1 pad_maximum_fusion.5
  327.2 0.7 gather_fusion.5
  327.9 3.5 %fusion.72 = bf16[6,256,128]{1,2,0:T(8,128)(2,1)S(1)} fusion(bf16[6,5,256,256]{3,2,1,0:T(8,128)(2,1)} %param.8, bf16[6,5,256,128]{2,3,1,0:T(8,128)(2,1)S(1)} %bitcast.123, pred[6,5]{1,0:T(8,128)(4,1)S(1)} %get-tuple-element.6, bf16[6,256,128]{1,2,0:T(8,128)(2,1)S(1)} %fusion.94), kind=kOutput, calls=%fused_computation.43 | convolution fusion | flops 505085952 | bytes 6684702 | tf_op jit(solution)/shard_map/esij,esjm->eim/dot_general | solution.py:28
  331.4 0.9 copy.16
  (8 shorter events, 0.2 us)
Async XLA Ops:
  6.5 241.4 %all-gather.2.cloned.1.call-start = ((), (), s32[]{:S(2)}) async-start(), calls=%async_computation.2 | async-start | bytes 2359296 | tf_op jit(solution)/shard_map/all_gather | solution.py:51
  7.6 153.8 %collective-permute-start = (bf16[3,256,128]{2,1,0:T(8,128)(2,1)S(1)}, bf16[3,256,128]{2,1,0:T(8,128)(2,1)S(1)}, u32[]{:S(2)}, u32[]{:S(2)}) collective-permute-start(bf16[3,256,128]{2,1,0:T(8,128)(2,1)S(1)} %get-tuple-element.18), channel_id=1, source_target_pairs={{0,8},{8,16},{16,24},{24,32},{32,40},{40,48},{48,56},{56,64},{64,7... | collective-permute-start | bytes 589832 | tf_op jit(solution)/shard_map/ppermute | solution.py:16
  12.4 149.0 %collective-permute-start.1 = (bf16[3,256,128]{2,1,0:T(8,128)(2,1)S(1)}, bf16[3,256,128]{2,1,0:T(8,128)(2,1)S(1)}, u32[]{:S(2)}, u32[]{:S(2)}) collective-permute-start(bf16[3,256,128]{2,1,0:T(8,128)(2,1)S(1)} %get-tuple-element.19), channel_id=1, source_target_pairs={{8,0},{16,8},{24,16},{32,24},{40,32},{48,40},{56,48},{64,56},{72,6... | collective-permute-start | bytes 589832 | tf_op jit(solution)/shard_map/ppermute | solution.py:18
  165.8 13.7 %copy-start = (bf16[6,256,128]{2,1,0:T(8,128)(2,1)S(1)}, bf16[6,256,128]{2,1,0:T(8,128)(2,1)}, u32[]{:S(2)}) copy-start(bf16[6,256,128]{2,1,0:T(8,128)(2,1)} %param.7) | copy-start | bytes 1179652
  170.0 10.6 %collective-permute-start.2 = (bf16[3,256,128]{1,2,0:T(8,128)(2,1)S(1)}, bf16[3,256,128]{1,2,0:T(8,128)(2,1)S(1)}, u32[]{:S(2)}, u32[]{:S(2)}) collective-permute-start(bf16[3,256,128]{1,2,0:T(8,128)(2,1)S(1)} %get-tuple-element.16), channel_id=1, source_target_pairs={{0,8},{8,16},{16,24},{24,32},{32,40},{40,48},{48,56},{56,64},{64,7... | collective-permute-start | bytes 589832 | tf_op jit(solution)/shard_map/ppermute | solution.py:16
  171.9 10.2 %collective-permute-start.3 = (bf16[3,256,128]{1,2,0:T(8,128)(2,1)S(1)}, bf16[3,256,128]{1,2,0:T(8,128)(2,1)S(1)}, u32[]{:S(2)}, u32[]{:S(2)}) collective-permute-start(bf16[3,256,128]{1,2,0:T(8,128)(2,1)S(1)} %get-tuple-element.17), channel_id=1, source_target_pairs={{8,0},{16,8},{24,16},{32,24},{40,32},{48,40},{56,48},{64,56},{72,6... | collective-permute-start | bytes 589832 | tf_op jit(solution)/shard_map/ppermute | solution.py:18
  186.4 11.1 %collective-permute-start.4 = (bf16[3,256,128]{1,2,0:T(8,128)(2,1)S(1)}, bf16[3,256,128]{1,2,0:T(8,128)(2,1)S(1)}, u32[]{:S(2)}, u32[]{:S(2)}) collective-permute-start(bf16[3,256,128]{1,2,0:T(8,128)(2,1)S(1)} %get-tuple-element.14), channel_id=1, source_target_pairs={{0,8},{8,16},{16,24},{24,32},{32,40},{40,48},{48,56},{56,64},{64,7... | collective-permute-start | bytes 589832 | tf_op jit(solution)/shard_map/ppermute | solution.py:16
  188.4 15.9 %collective-permute-start.5 = (bf16[3,256,128]{1,2,0:T(8,128)(2,1)S(1)}, bf16[3,256,128]{1,2,0:T(8,128)(2,1)S(1)}, u32[]{:S(2)}, u32[]{:S(2)}) collective-permute-start(bf16[3,256,128]{1,2,0:T(8,128)(2,1)S(1)} %get-tuple-element.15), channel_id=1, source_target_pairs={{8,0},{16,8},{24,16},{32,24},{40,32},{48,40},{56,48},{64,56},{72,6... | collective-permute-start | bytes 589832 | tf_op jit(solution)/shard_map/ppermute | solution.py:18
  205.1 42.8 %copy-start.1 = (s32[1024]{0:T(1024)S(1)}, s32[1024]{0:T(1024)}, u32[]{:S(2)}) copy-start(s32[1024]{0:T(1024)} %param.10) | copy-start | bytes 12292
  209.6 50.7 %all-to-all-start = ((bf16[8,192,128]{2,1,0:T(8,128)(2,1)}), bf16[8,192,128]{2,1,0:T(8,128)(2,1)S(1)}, u32[]{:S(2)}, u32[]{:S(2)}) async-start(bf16[8,192,128]{2,1,0:T(8,128)(2,1)} %bitcast.12), calls=%async_computation | async-start | bytes 786432 | tf_op jit(solution)/shard_map/all_to_all | solution.py:54
  276.0 12.9 %collective-permute-start.6 = (bf16[3,256,128]{2,1,0:T(8,128)(2,1)S(1)}, bf16[3,256,128]{2,1,0:T(8,128)(2,1)S(1)}, u32[]{:S(2)}, u32[]{:S(2)}) collective-permute-start(bf16[3,256,128]{2,1,0:T(8,128)(2,1)S(1)} %bitcast.129), channel_id=1, source_target_pairs={{0,8},{8,16},{16,24},{24,32},{32,40},{40,48},{48,56},{56,64},{64,7... | collective-permute-start | bytes 589832 | tf_op jit(solution)/shard_map/ppermute | solution.py:16
  278.0 11.9 %collective-permute-start.7 = (bf16[3,256,128]{2,1,0:T(8,128)(2,1)S(1)}, bf16[3,256,128]{2,1,0:T(8,128)(2,1)S(1)}, u32[]{:S(2)}, u32[]{:S(2)}) collective-permute-start(bf16[3,256,128]{2,1,0:T(8,128)(2,1)S(1)} %bitcast.128), channel_id=1, source_target_pairs={{8,0},{16,8},{24,16},{32,24},{40,32},{48,40},{56,48},{64,56},{72,6... | collective-permute-start | bytes 589832 | tf_op jit(solution)/shard_map/ppermute | solution.py:18
  297.4 11.4 %collective-permute-start.8 = (bf16[3,256,128]{1,2,0:T(8,128)(2,1)S(1)}, bf16[3,256,128]{1,2,0:T(8,128)(2,1)S(1)}, u32[]{:S(2)}, u32[]{:S(2)}) collective-permute-start(bf16[3,256,128]{1,2,0:T(8,128)(2,1)S(1)} %get-tuple-element.10), channel_id=1, source_target_pairs={{0,8},{8,16},{16,24},{24,32},{32,40},{40,48},{48,56},{56,64},{64,7... | collective-permute-start | bytes 589832 | tf_op jit(solution)/shard_map/ppermute | solution.py:16
  299.3 10.9 %collective-permute-start.9 = (bf16[3,256,128]{1,2,0:T(8,128)(2,1)S(1)}, bf16[3,256,128]{1,2,0:T(8,128)(2,1)S(1)}, u32[]{:S(2)}, u32[]{:S(2)}) collective-permute-start(bf16[3,256,128]{1,2,0:T(8,128)(2,1)S(1)} %get-tuple-element.11), channel_id=1, source_target_pairs={{8,0},{16,8},{24,16},{32,24},{40,32},{48,40},{56,48},{64,56},{72,6... | collective-permute-start | bytes 589832 | tf_op jit(solution)/shard_map/ppermute | solution.py:18
  314.6 11.1 %collective-permute-start.10 = (bf16[3,256,128]{1,2,0:T(8,128)(2,1)S(1)}, bf16[3,256,128]{1,2,0:T(8,128)(2,1)S(1)}, u32[]{:S(2)}, u32[]{:S(2)}) collective-permute-start(bf16[3,256,128]{1,2,0:T(8,128)(2,1)S(1)} %get-tuple-element.8), channel_id=1, source_target_pairs={{0,8},{8,16},{16,24},{24,32},{32,40},{40,48},{48,56},{56,64},{64,7... | collective-permute-start | bytes 589832 | tf_op jit(solution)/shard_map/ppermute | solution.py:16
  316.5 10.6 %collective-permute-start.11 = (bf16[3,256,128]{1,2,0:T(8,128)(2,1)S(1)}, bf16[3,256,128]{1,2,0:T(8,128)(2,1)S(1)}, u32[]{:S(2)}, u32[]{:S(2)}) collective-permute-start(bf16[3,256,128]{1,2,0:T(8,128)(2,1)S(1)} %get-tuple-element.9), channel_id=1, source_target_pairs={{8,0},{16,8},{24,16},{32,24},{40,32},{48,40},{56,48},{64,56},{72,6... | collective-permute-start | bytes 589832 | tf_op jit(solution)/shard_map/ppermute | solution.py:18
Sparse Core Ops, SparseCore 0:
  160.8 64.8 all-gather.1
where the time goes:
time: 341 us; the launch traced here: 339 us
  blocking collectives  152 us (45%)
  starting transfers between devices  106 us (31%)
  waiting for transfers between devices  23.9 us (7%)
  matrix products  22.9 us (7%)
  local copies, waits for them, and re-layouts  19.3 us (6%)
  between operations  13.7 us (4%)
    all_gather x1, blocking collectives, body(): rotation_cols = lax.all_gather(rotation, 'elem', axis=0, tiled=True)  136 us
    ppermute x6, starting transfers between devices, extended_2(): lax.ppermute(head, axis, [((i + 1) % count, i) for i in range(count)])  52.8 us
    all_to_all x1, starting transfers between devices, body(): lax.all_to_all(flat_rows, 'band', split_axis=0, concat_axis=1, tiled=True)  38.3 us
    dot_general x6, matrix products, apply_blocks(): jnp.einsum('esij,esjm->eim', blocks, picked, preferred_element_type=jnp.f...  22.4 us
    all_to_all x1, blocking collectives, body(): lax.all_to_all(mixed_rows, 'band', split_axis=1, concat_axis=0, tiled=True)  15.1 us
    ppermute x6, starting transfers between devices, extended_2(): lax.ppermute(tail, axis, [(i, (i + 1) % count) for i in range(count)])  14.4 us
    ppermute x6, waiting for transfers between devices, extended_2(): lax.ppermute(head, axis, [((i + 1) % count, i) for i in range(count)])  12.1 us
    gather x8, local copies, waits for them, and re-layouts, apply_blocks(): picked = jnp.take(extended, local_links, axis=0)  9.16 us
  transfers between devices with their start and end apart: 14, of which 11 were waited for; matrix products, arithmetic and copies ran while one was open for 8% of the time, Pallas kernels for 0%

commit v1 on v0

v1 whole, which is shorter than its diff:
```python
import functools

import jax
import jax.numpy as jnp
from jax import lax
from jax.experimental import pallas as pl
from jax.experimental.pallas import tpu as pltpu
from jax.sharding import PartitionSpec as P

MESH = pl.DeviceIdType.MESH
GY = 3
LANES = 128
SIZES = dict(X=4, YL=2, Z=8, YH=4)


def kernel(X, YL, Z, YH, start, blocks, links, order, rotation, out, blk, perm, rot, rotp, racc, *rest):
    bf16, f32 = jnp.bfloat16, jnp.float32
    rest = list(rest)

    def take(n):
        got, rest[:] = rest[:n], rest[n:]
        return got

    own = [take(2) for _ in range(6)]
    near = [take(2) for _ in range(6)]
    far = [take(2) for _ in range(6)]
    acc = take(2)
    filt = [take(2) for _ in range(2)]
    gath = take(2)
    back = take(2)
    (s_blk, s_init, r_own, s_halo, r_halo, s_rot, r_rot, l_rot, s_a2a, r_a2a, l_a2a, s_out, r_out, l_out) = rest

    E = X * YL * Z
    Y = YH * YL
    nb = blk.shape[2]
    part = nb // YH
    elem, band = lax.axis_index("elem"), lax.axis_index("band")
    core, yh = band % 2, band // 2
    z, yl, x = elem % Z, (elem // Z) % YL, elem // (Z * YL)
    y = yh * YL + yl
    partner = (elem, yh * 2 + 1 - core)
    zelem = (elem - 1 + 2 * core + E) % E
    zpeer = (zelem, yh * 2 + 1 - core)
    zother = ((elem + 1 - 2 * core + E) % E, band)
    mine, theirs = GY * core, GY * (1 - core)

    def remote(src, dst, ss, rs, dev):
        return pltpu.make_async_remote_copy(
            src_ref=src, dst_ref=dst, send_sem=ss, recv_sem=rs, device_id=dev, device_id_type=MESH
        )

    def wait(ref, sem):
        pltpu.make_async_copy(ref, ref, sem).wait()

    for i in range(GY):
        pltpu.make_async_copy(blocks.at[mine + i], blk.at[i], s_blk.at[i]).start()
    pltpu.make_async_copy(rotation, rot.at[core, x, y, z], l_rot).start()
    for k in range(2):

        @pl.when(core == k)
        def _():
            pltpu.make_async_copy(start.at[pl.ds(mine, GY)], own[0][k], r_own.at[k]).start()
            pltpu.make_async_copy(start.at[pl.ds(theirs, GY)], near[0][k], r_halo.at[0, k, 0]).start()

    z_peers = [(elem - z + (z + d) % Z, band) for d in range(1, Z)]
    y_peers = []
    for d in range(1, Y):
        other = (y + d) % Y
        y_peers.append(((x * YL + other % YL) * Z + z, (other // YL) * 2 + core))
    x_peers = [((((x + d) % X) * YL + yl) * Z + z, band) for d in range(1, X)]
    a_peers = [(elem, ((yh + d) % YH) * 2 + core) for d in range(1, YH)]

    barrier = pltpu.get_barrier_semaphore()
    greeted = [partner] + z_peers + y_peers + x_peers
    for step in (1, E - 1):
        for c in range(2):
            greeted.append(((elem + step) % E, yh * 2 + c))
    for dev in greeted:
        pl.semaphore_signal(barrier, inc=1, device_id=dev, device_id_type=MESH)
    pl.semaphore_wait(barrier, len(greeted))

    for k in range(2):
        sends = [
            remote(start.at[pl.ds(mine, GY)], far[0][k], s_init.at[0], r_halo.at[0, k, 1], zpeer),
            remote(start.at[pl.ds(theirs, GY)], far[0][k], s_init.at[1], r_halo.at[0, k, 1], zother),
            remote(start.at[pl.ds(theirs, GY)], own[0][k], s_init.at[2], r_own.at[k], partner),
            remote(start.at[pl.ds(mine, GY)], near[0][k], s_init.at[3], r_halo.at[0, k, 0], partner),
        ]

        @pl.when(core == k)
        def _():
            for copy in sends:
                copy.start()

    for dev in z_peers:
        remote(rotation, rot.at[core, x, y, z], s_rot.at[0], r_rot.at[0], dev).start()

    kts, width = perm.shape[0], perm.shape[3]

    def one_hot(step, carry):
        kt, xx = step // X, step % X
        k, yp = kt // (YH // 2), kt % (YH // 2)
        for h in range(2):
            rows = lax.broadcasted_iota(jnp.int32, (LANES, LANES), 0) + ((2 * yp + h) * 2 + k) * LANES
            for j in range(width // LANES):
                wanted = order[pl.ds(xx * (width // LANES) + j, 1), :]
                hit = jnp.where(rows == wanted, 1.0, 0.0).astype(bf16)
                perm[kt, xx, h * LANES : (h + 1) * LANES, j * LANES : (j + 1) * LANES] = hit
        return carry

    lax.fori_loop(0, kts * X, one_hot, 0)

    t_near, t_far = 2 - core, 1 + core

    def before(st, k):
        def one(i, carry):
            row = mine + i
            total = jnp.dot(blk[i, t_near], near[st][k][lax.rem(links[row, t_near], GY)], preferred_element_type=f32)
            for t in (0, 3, 4):
                total += jnp.dot(blk[i, t], own[st][k][lax.rem(links[row, t], GY)], preferred_element_type=f32)
            acc[k][i] = total
            return carry

        lax.fori_loop(0, GY, one, 0)

    def halo(st, k, i):
        src = own[st][k].at[i]
        return (
            remote(src, far[st][k].at[i], s_halo.at[st, k, 1], r_halo.at[st, k, 1], zpeer),
            remote(src, near[st][k].at[i], s_halo.at[st, k, 0], r_halo.at[st, k, 0], partner),
        )

    def after(st, k):
        f, last = st // 3, st % 3 == 2

        def one(i, carry):
            row = mine + i
            total = acc[k][i] + jnp.dot(
                blk[i, t_far], far[st][k][lax.rem(links[row, t_far], GY)], preferred_element_type=f32
            )
            if st % 3:
                total = 2.0 * total - own[st - 1][k][i].astype(f32)
            (filt[f] if last else own[st + 1])[k][i] = total.astype(bf16)
            if not last:
                for copy in halo(st + 1, k, i):
                    copy.start()
            return carry

        lax.fori_loop(0, GY, one, 0)

    def exchange(k, d):
        q = (yh + d) % YH
        return remote(
            filt[0][k].at[:, pl.ds(q * part, part), :], gath[k].at[yh], s_a2a.at[0, k], r_a2a.at[0, k], a_peers[d - 1]
        )

    def give_back(k, d):
        q = (yh + d) % YH
        return remote(
            back[k].at[q], own[3][k].at[:, pl.ds(yh * part, part), :], s_a2a.at[1, k], r_a2a.at[1, k], a_peers[d - 1]
        )

    for k in range(2):
        wait(own[0][k], r_own.at[k])
        wait(near[0][k], r_halo.at[0, k, 0])
        if k == 0:
            for i in range(GY):
                wait(blk.at[i], s_blk.at[i])
        before(0, k)
    for k in range(2):
        wait(far[0][k], r_halo.at[0, k, 1])
        after(0, k)
    wait(rot.at[core, x, y, z], l_rot)
    wait(rot.at[core, x, y, pl.ds(0, Z - 1)], r_rot.at[0])
    for dev in y_peers:
        remote(rot.at[core, x, y], rot.at[core, x, y], s_rot.at[1], r_rot.at[1], dev).start()
    for st in (1, 2):
        for k in range(2):
            wait(near[st][k], r_halo.at[st, k, 0])
            before(st, k)
        for k in range(2):
            wait(far[st][k], r_halo.at[st, k, 1])
            after(st, k)
            if st == 2:
                for d in range(1, YH):
                    exchange(k, d).start()
                mine_part = filt[0][k].at[:, pl.ds(yh * part, part), :]
                pltpu.make_async_copy(mine_part, gath[k].at[yh], l_a2a.at[0, k]).start()
        if st == 1:
            wait(rot.at[core, x, pl.ds(0, Y - 1)], r_rot.at[1])
            for dev in x_peers:
                remote(rot.at[core, x], rot.at[core, x], s_rot.at[2], r_rot.at[2], dev).start()

    wait(rot.at[core, pl.ds(0, X - 1)], r_rot.at[2])
    swap = remote(rot.at[core], rot.at[core], s_rot.at[3], r_rot.at[3], partner)
    swap.start()
    wait(rot.at[core], r_rot.at[3])
    half = YH // 2

    def permute(step, carry):
        kt, nt = step // kts, step % kts
        k, yp = nt // half, nt % half
        total = None
        for xx in range(X):
            sides = [rot[k, xx, pl.ds((2 * yp + h) * YL, YL)].reshape(width, LANES) for h in range(2)]
            term = jnp.dot(perm[kt, xx], jnp.concatenate(sides, axis=1), preferred_element_type=f32)
            total = term if total is None else total + term
        rotp[kt, nt] = total.astype(bf16)
        return carry

    lax.fori_loop(0, kts * kts, permute, 0)

    def product(k, nt):
        total = None
        for yp in range(half):
            sides = [gath[k][2 * yp + h].reshape(GY * part, LANES) for h in range(2)]
            term = jnp.dot(jnp.concatenate(sides, axis=1), rotp[k * half + yp, nt], preferred_element_type=f32)
            total = term if total is None else total + term
        return total

    for k in range(2):
        wait(gath[k].at[0], l_a2a.at[0, k])
        wait(gath[k].at[pl.ds(0, YH - 1)], r_a2a.at[0, k])
        if k == 0:

            def partial(nt, carry):
                racc[nt] = product(0, nt)
                return carry

            lax.fori_loop(0, kts, partial, 0)
    for k in range(2):

        def finish(yp, carry):
            total = (racc[k * half + yp] + product(1, k * half + yp)).astype(bf16)
            for h in range(2):
                back[k][2 * yp + h] = total[:, h * LANES : (h + 1) * LANES].reshape(GY, part, LANES)
            return carry

        lax.fori_loop(0, half, finish, 0)
        for d in range(1, YH):
            give_back(k, d).start()
        pltpu.make_async_copy(back[k].at[yh], own[3][k].at[:, pl.ds(yh * part, part), :], l_a2a.at[1, k]).start()

    for k in range(2):
        wait(gath[k].at[0], l_a2a.at[1, k])
        wait(gath[k].at[pl.ds(0, YH - 1)], r_a2a.at[1, k])
        for i in range(GY):
            for copy in halo(3, k, i):
                copy.start()
        wait(near[3][k], r_halo.at[3, k, 0])
        before(3, k)
    for st in (3, 4, 5):
        if st > 3:
            for k in range(2):
                wait(near[st][k], r_halo.at[st, k, 0])
                before(st, k)
        for k in range(2):
            wait(far[st][k], r_halo.at[st, k, 1])
            after(st, k)
            if st == 5:
                here = out.at[pl.ds(mine, GY)]

                @pl.when(core == k)
                def _():
                    pltpu.make_async_copy(filt[1][k], here, l_out).start()

                @pl.when(core != k)
                def _():
                    remote(filt[1][k], here, s_out, r_out, partner).start()

    wait(out.at[pl.ds(mine, GY)], l_out)
    wait(out.at[pl.ds(theirs, GY)], r_out)
    wait(filt[1][0], s_out)
    for j in range(4):
        wait(own[0][0], s_init.at[j])
    for st in range(1, 6):
        for k in range(2):
            for side in range(2):
                wait(own[st][k], s_halo.at[st, k, side])
    wait(rot.at[core, x, y, pl.ds(0, Z - 1)], s_rot.at[0])
    wait(rot.at[core, x, pl.ds(0, Y - 1)], s_rot.at[1])
    wait(rot.at[core, pl.ds(0, X - 1)], s_rot.at[2])
    wait(rot.at[core], s_rot.at[3])
    for j in range(2):
        for k in range(2):
            wait(gath[k].at[pl.ds(0, YH - 1)], s_a2a.at[j, k])


def build(mesh, X, YL, Z, YH):
    Y = YH * YL

    def body(start, blocks, neighbours, band_order, rotation):
        nb = start.shape[1]
        bands = band_order.shape[0]
        rows = rotation.shape[0]
        part = nb // YH
        kts = YH
        bf16 = jnp.bfloat16
        column = pltpu.VMEM((GY, nb, LANES), bf16)
        dma = pltpu.SemaphoreType.DMA
        hbm = pl.BlockSpec(memory_space=pl.ANY)
        return pl.pallas_call(
            functools.partial(kernel, X, YL, Z, YH),
            out_shape=jax.ShapeDtypeStruct(start.shape, bf16),
            in_specs=[
                hbm,
                hbm,
                pl.BlockSpec(memory_space=pltpu.SMEM),
                pl.BlockSpec(memory_space=pltpu.VMEM),
                hbm,
            ],
            out_specs=hbm,
            scratch_shapes=[
                pltpu.VMEM((GY, 5, nb, nb), bf16),
                pltpu.VMEM((kts, X, 2 * LANES, bands // X), bf16),
                pltpu.VMEM((2, X, Y, Z, rows, LANES), bf16),
                pltpu.VMEM((kts, kts, 2 * LANES, 2 * LANES), bf16),
                pltpu.VMEM((kts, GY * part, 2 * LANES), jnp.float32),
                *[column] * 36,
                *[pltpu.VMEM((GY, nb, LANES), jnp.float32)] * 2,
                *[column] * 4,
                *[pltpu.VMEM((YH, GY, part, LANES), bf16)] * 4,
                dma((GY,)),
                dma((4,)),
                dma((2,)),
                dma((6, 2, 2)),
                dma((6, 2, 2)),
                dma((4,)),
                dma((4,)),
                dma,
                dma((2, 2)),
                dma((2, 2)),
                dma((2, 2)),
                dma,
                dma,
                dma,
            ],
            compiler_params=pltpu.CompilerParams(collective_id=0, has_side_effects=True),
        )(start, blocks, neighbours, band_order.reshape(bands // LANES, LANES), rotation)

    return jax.shard_map(
        body,
        mesh=mesh,
        in_specs=(
            P("elem", None, "band"),
            P("elem", None, None, None),
            P("elem", None),
            P(),
            P("elem", "band"),
        ),
        out_specs=P("elem", None, "band"),
        check_vma=False,
    )


def solution(mesh):
    return build(mesh, **SIZES)
```

time: 341 us -> 91.5 us (0.27)
  blocking collectives: 152 us -> 0 us
  starting transfers between devices: 106 us -> 0 us
  Pallas kernels: 0 us -> 89.6 us
  waiting for transfers between devices: 23.9 us -> 0 us
  matrix products: 22.9 us -> 0 us
  local copies, waits for them, and re-layouts: 19.3 us -> 1.77 us
  between operations: 13.7 us -> 0.01 us
    all_gather x1 -> x0, blocking collectives: 136 us -> none  [body(): rotation_cols = lax.all_gather(rotation, 'elem', axis=0, tiled=True)]
    pallas_call x0 -> x1, Pallas kernels: none -> 89.6 us  [body(): pl.pallas_call(functools.partial(kernel, X, YL, Z, YH), out_shape=jax.Sha...]
    ppermute x12 -> x0, starting transfers between devices: 67.3 us -> none  [the longest x6 52.8 us: extended_2(): lax.ppermute(head, axis, [((i + 1) % count, i) for i in range(count)])]
    all_to_all x1 -> x0, starting transfers between devices: 38.3 us -> none  [body(): lax.all_to_all(flat_rows, 'band', split_axis=0, concat_axis=1, tiled=True)]
    dot_general x7 -> x0, matrix products: 22.9 us -> none  [the longest x6 22.4 us: apply_blocks(): jnp.einsum('esij,esjm->eim', blocks, picked, preferred_element_type=jnp.f...]
    ppermute x12 -> x0, waiting for transfers between devices: 18.2 us -> none  [the longest x6 12.1 us: extended_2(): lax.ppermute(head, axis, [((i + 1) % count, i) for i in range(count)])]
    all_to_all x1 -> x0, blocking collectives: 15.1 us -> none  [body(): lax.all_to_all(mixed_rows, 'band', split_axis=1, concat_axis=0, tiled=True)]
    gather x8 -> x0, local copies, waits for them, and re-layouts: 9.16 us -> none  [apply_blocks(): picked = jnp.take(extended, local_links, axis=0)]
  transfers between devices with their start and end apart: 14 -> 0, of which waited for: 11 -> 0; matrix products, arithmetic and copies ran while one was open for 8% -> 0% of each run, Pallas kernels for 0% -> 0%
where the time goes in v1:
time: 91.5 us; the launch traced here: 91.4 us
  Pallas kernels  89.6 us (98%)
  local copies, waits for them, and re-layouts  1.77 us (2%)
    pallas_call x1, Pallas kernels, body(): pl.pallas_call(functools.partial(kernel, X, YL, Z, YH), out_shape=jax.Sha...  89.6 us

profile of v1, /device:TPU:1, one launch (start us, length us, event | category | flops | bytes accessed | tf_op | source)
XLA Modules:
  0.0 91.4 jit_solution(13385520821618912842)
XLA Ops:
  0.0 89.6 %shard_map.55 = bf16[6,256,128]{2,1,0:T(8,128)(2,1)} custom-call(bf16[6,256,128]{2,1,0:T(8,128)(2,1)} %start.1, bf16[6,5,256,256]{3,2,1,0:T(8,128)(2,1)} %blocks.1, s32[6,5]{1,0:T(8,128)} %links.1, s32[8,128]{1,0:T(8,128)} %bitcast.1, bf16[16,128]{1,0:T(8,128)(2,1)} %rotation.1), custom_call_target="tpu_custom_call" | custom-call | tf_op jit(solution)/shard_map/pallas_call | solution.py:302
  89.6 1.8 %copy.7 = bf16[6,256,128]{2,1,0:T(8,128)(2,1)} copy(bf16[6,256,128]{2,1,0:T(8,128)(2,1)} %shard_map.55) | data formatting | bytes 786432

commit v2 on v0

v2 whole, which is shorter than its diff:
```python
import functools

import jax
import jax.numpy as jnp
from jax import lax
from jax.experimental import pallas as pl
from jax.experimental.pallas import tpu as pltpu
from jax.sharding import PartitionSpec as P

MESH = pl.DeviceIdType.MESH
GY = 3
LANES = 128
SIZES = dict(X=4, YL=2, Z=8, YH=4)


def kernel(X, YL, Z, YH, start, blocks, links_in, order_in, rotation, out, blk, perm, rot, racc, turned, links, table, order, *rest):
    bf16, f32 = jnp.bfloat16, jnp.float32
    rest = list(rest)

    def take(n):
        got, rest[:] = rest[:n], rest[n:]
        return got

    own = [take(2) for _ in range(6)]
    near = [take(2) for _ in range(6)]
    far = [take(2) for _ in range(6)]
    acc = take(2)
    filt = take(2)
    gath = take(2)
    back = take(2)
    (
        (s_blk, s_small, s_init, r_own, s_near, r_near, s_far, r_far),
        (s_z, r_z, l_rot, s_y, r_y, s_slab, r_slab, s_x, r_x, s_core, r_core),
        (s_a2a, r_a2a, l_a2a, s_out, r_out, l_out),
    ) = rest[:8], rest[8:19], rest[19:]

    E = X * YL * Z
    Y = YH * YL
    nb = blk.shape[2]
    part = nb // YH
    half = YH // 2
    elem, band = lax.axis_index("elem"), lax.axis_index("band")
    core, yh = lax.rem(band, 2), lax.div(band, 2)
    z, yl, x = lax.rem(elem, Z), lax.rem(lax.div(elem, Z), YL), lax.div(elem, Z * YL)
    y = yh * YL + yl
    twin = yh * 2 + 1 - core
    partner = (elem, twin)
    zpeer = (lax.rem(elem - 1 + 2 * core + E, E), twin)
    zother = (lax.rem(elem + 1 - 2 * core + E, E), band)
    mine, theirs = GY * core, GY * (1 - core)

    def remote(src, dst, ss, rs, dev):
        return pltpu.make_async_remote_copy(
            src_ref=src, dst_ref=dst, send_sem=ss, recv_sem=rs, device_id=dev, device_id_type=MESH
        )

    def wait(ref, sem):
        pltpu.make_async_copy(ref, ref, sem).wait()

    z_peers = [(elem - z + lax.rem(z + d, Z), band) for d in range(1, Z)]
    y_peers = []
    for d in range(1, Y):
        other = lax.rem(y + d, Y)
        y_peers.append(((x * YL + lax.rem(other, YL)) * Z + z, lax.div(other, YL) * 2 + core))
    x_peers = [((lax.rem(x + d, X) * YL + yl) * Z + z, band) for d in range(1, X)]
    a_peers = [(elem, lax.rem(yh + d, YH) * 2 + core) for d in range(1, YH)]

    barrier = pltpu.get_barrier_semaphore()
    greeted = [partner] + z_peers + y_peers + x_peers
    greeted += [(elem, lax.rem(yh + d, YH) * 2 + 1 - core) for d in range(1, YH)]
    for step in (1, E - 1):
        for c in range(2):
            greeted.append((lax.rem(elem + step, E), yh * 2 + c))
    for dev in greeted:
        pl.semaphore_signal(barrier, inc=1, device_id=dev, device_id_type=MESH)

    pltpu.make_async_copy(links_in, links, s_small.at[0]).start()
    pltpu.make_async_copy(order_in, order, s_small.at[1]).start()
    for k in range(2):

        @pl.when(core == k)
        def _():
            pltpu.make_async_copy(start.at[pl.ds(mine, GY)], own[0][k], r_own.at[k]).start()
            pltpu.make_async_copy(start.at[pl.ds(theirs, GY)], near[0][k], r_near.at[0, k]).start()

    for i in range(GY):
        pltpu.make_async_copy(blocks.at[mine + i], blk.at[i], s_blk.at[i]).start()
    pl.semaphore_wait(barrier, len(greeted))

    def at_end(c):
        return jnp.logical_or(c == 0, c == Z - 1)

    end_plane = at_end(z)
    inner_plane = jnp.logical_not(end_plane)

    @pl.when(inner_plane)
    def _():
        pltpu.make_async_copy(rotation, rot.at[core, x, y, z], l_rot).start()

    for d, dev in enumerate(z_peers):

        @pl.when(jnp.logical_not(at_end(lax.rem(z + d + 1, Z))))
        def _():
            remote(rotation, rot.at[core, x, y, z], s_z, r_z, dev).start()

    def first_far(k):
        remote(start.at[pl.ds(mine, GY)], far[0][k], s_init.at[0], r_far.at[0, k, 0], zpeer).start()
        remote(start.at[pl.ds(theirs, GY)], far[0][k], s_init.at[1], r_far.at[0, k, 0], zother).start()

    for k in range(2):

        @pl.when(core == k)
        def _():
            first_far(k)
            remote(start.at[pl.ds(theirs, GY)], own[0][k], s_init.at[2], r_own.at[k], partner).start()
            remote(start.at[pl.ds(mine, GY)], near[0][k], s_init.at[3], r_near.at[0, k], partner).start()

    wait(links, s_small.at[0])
    wait(order, s_small.at[1])
    t_near, t_far = 2 - core, 1 + core

    def place(row, t):
        return lax.rem(links[row, t], GY)

    def slot_of(c, e):
        return jnp.where(c == 1, place(GY + e, 2), e)

    for j in range(GY):
        e = jnp.where(
            core == 0,
            j,
            jnp.where(place(GY, 2) == j, 0, jnp.where(place(GY + 1, 2) == j, 1, 2)),
        )
        for v, at in ((0, e), (1, e), (2, j)):
            row = mine + at
            ids = (place(row, 3), place(row, 4), place(row, t_near), place(row, t_far))
            if v == 0:
                line = (at, at, *ids)
            else:
                here = j if v == 1 else slot_of(core, at)
                line = (at, here, slot_of(core, ids[0]), slot_of(core, ids[1]), slot_of(1 - core, ids[2]), here)
            for n, value in enumerate(line):
                table[v, j * 6 + n] = value

    kts, width = perm.shape[0], perm.shape[3]

    def one_hot(step, carry):
        kt, xx = lax.div(step, X), lax.rem(step, X)
        k, yp = lax.div(kt, half), lax.rem(kt, half)
        for h in range(2):
            rows = lax.broadcasted_iota(jnp.int32, (LANES, LANES), 0) + ((2 * yp + h) * 2 + k) * LANES
            for j in range(width // LANES):
                wanted = order[pl.ds(xx * (width // LANES) + j, 1), :]
                hit = jnp.where(rows == wanted, 1.0, 0.0).astype(bf16)
                perm[kt, xx, h * LANES : (h + 1) * LANES, j * LANES : (j + 1) * LANES] = hit
        return carry

    def row_of(st):
        return 0 if st == 0 else 2 if st == 5 else 1

    def before(st, k):
        v = row_of(st)

        def one(j, carry):
            e = table[v, j * 6]
            total = jnp.dot(blk[e, t_near], near[st][k][table[v, j * 6 + 4]], preferred_element_type=f32)
            for n, t in ((1, 0), (2, 3), (3, 4)):
                total += jnp.dot(blk[e, t], own[st][k][table[v, j * 6 + n]], preferred_element_type=f32)
            acc[k][j] = total
            return carry

        lax.fori_loop(0, GY, one, 0)

    def halo(st, k, j):
        src = own[st][k].at[j]
        remote(src, far[st][k].at[j], s_far.at[st, k], r_far.at[st, k, j], zpeer).start()
        remote(src, near[st][k].at[j], s_near.at[st, k], r_near.at[st, k], partner).start()

    def exchange(k, j):
        for d in range(1, YH):
            q = lax.rem(yh + d, YH)
            src = filt[k].at[j, pl.ds(q * part, part)]
            remote(src, gath[k].at[yh, j], s_a2a.at[k], r_a2a.at[k], a_peers[d - 1]).start()
        src = filt[k].at[j, pl.ds(yh * part, part)]
        pltpu.make_async_copy(src, gath[k].at[yh, j], l_a2a.at[k]).start()

    def after(st, k):
        v = row_of(st)
        if st == 0:
            wait(far[0][k], r_far.at[0, k, 0])
        if st == 5:
            for j in range(GY):
                wait(far[st][k].at[j], r_far.at[st, k, j])

        def one(j, carry):
            e = table[v, j * 6]
            if st in (0, 5):
                there = far[st][k][table[v, j * 6 + 5]]
            else:
                wait(far[st][k].at[j], r_far.at[st, k, j])
                there = far[st][k][j]
            total = acc[k][j] + jnp.dot(blk[e, t_far], there, preferred_element_type=f32)
            if st % 3:
                previous = own[st - 1][k][e if st == 1 else table[v, j * 6 + 1]]
                total = 2.0 * total - previous.astype(f32)
            if st < 5:
                own[st + 1][k][j] = total.astype(bf16)
                halo(st + 1, k, j)
            else:
                filt[k][j] = total.astype(bf16)
                exchange(k, j)
            return carry

        lax.fori_loop(0, GY, one, 0)

    def early(st, k):
        wait(near[st][k], r_near.at[st, k])
        before(st, k)

    lax.fori_loop(0, kts * X, one_hot, 0)
    wait(own[0][0], r_own.at[0])
    wait(near[0][0], r_near.at[0, 0])

    for i in range(GY):
        wait(blk.at[i], s_blk.at[i])
    before(0, 0)
    wait(own[0][1], r_own.at[1])
    early(0, 1)

    slab = rot.at[core, x]

    def along_y():
        wait(rot.at[core, x, y, z], l_rot)
        wait(rot.at[core, x, y, pl.ds(0, Z - 1)], r_z)
        at = rot.at[core, x, y]
        for d in range(1, Y):
            remote(at, at, s_y, r_y, y_peers[d - 1]).start()

    def along_x():
        for d in range(1, X):
            remote(slab, slab, s_x, r_x.at[d - 1], x_peers[d - 1]).start()
        remote(slab, slab, s_core, r_core.at[0], partner).start()

    pieces = [(yy, d) for yy in range(Y) for d in range(1, X)]

    def along_x_in_turn(turn, turns):
        @pl.when(end_plane)
        def _():
            if turn == 0:
                wait(slab, r_slab)
                remote(slab, slab, s_core, r_core.at[0], partner).start()
            for yy, d in pieces[turn * len(pieces) // turns : (turn + 1) * len(pieces) // turns]:
                at = rot.at[core, x, yy]
                remote(at, at, s_x, r_x.at[d - 1], x_peers[d - 1]).start()

    def hand_over():
        for d in range(1, X):
            at = rot.at[core, lax.rem(x - d + X, X)]
            wait(at, r_x.at[d - 1])
            remote(at, at, s_core, r_core.at[d], partner).start()

    for st in range(6):
        after(st, 0)
        if st == 0:
            pl.when(inner_plane)(along_y)
        if st == 1:

            @pl.when(inner_plane)
            def _():
                wait(rot.at[core, x, pl.ds(0, Y - 1)], r_y)

                @pl.when(z == 1)
                def _():
                    remote(slab, slab, s_slab.at[0], r_slab, (elem - 1, band)).start()

                @pl.when(z == Z - 2)
                def _():
                    remote(slab, slab, s_slab.at[1], r_slab, (elem + 1, band)).start()

                along_x()

        turn = 4 * (st - 2)
        if 2 <= st < 5:
            along_x_in_turn(turn, 12)
        if st == 4:
            pl.when(inner_plane)(hand_over)
        if st:
            early(st, 1)
        if 2 <= st < 5:
            along_x_in_turn(turn + 1, 12)
        after(st, 1)
        if 2 <= st < 5:
            along_x_in_turn(turn + 2, 12)
        if st < 5:
            early(st + 1, 0)
        if 2 <= st < 5:
            along_x_in_turn(turn + 3, 12)
    pl.when(end_plane)(hand_over)

    def reordered(k, xx):
        total = None
        for yp in range(half):
            sides = [gath[k][2 * yp + h].reshape(GY * part, LANES) for h in range(2)]
            term = jnp.dot(jnp.concatenate(sides, axis=1), perm[k * half + yp, xx], preferred_element_type=f32)
            total = term if total is None else total + term
        return total

    def first_half(xx, carry):
        racc[xx] = reordered(0, xx)
        return carry

    def second_half(xx, carry):
        turned[xx] = (racc[xx] + reordered(1, xx)).astype(bf16)
        return carry

    for k in range(2):
        wait(gath[k].at[0], l_a2a.at[k])
        wait(gath[k].at[pl.ds(0, YH - 1)], r_a2a.at[k])
        if k == 0:
            lax.fori_loop(0, X, first_half, 0)
    lax.fori_loop(0, X, second_half, 0)
    for d in range(X):
        wait(rot.at[core, 0], r_core.at[d])
    for k in range(2):
        for t in range(half):
            yp = lax.rem(lax.div(yh, 2) + 1 + t, half)
            total = None
            for xx in range(X):
                sides = [rot[k, xx, pl.ds((2 * yp + h) * YL, YL)].reshape(width, LANES) for h in range(2)]
                term = jnp.dot(turned[xx], jnp.concatenate(sides, axis=1), preferred_element_type=f32)
                total = term if total is None else total + term
            total = total.astype(bf16)
            for h in range(2):
                back[k][2 * yp + h] = total[:, h * LANES : (h + 1) * LANES].reshape(GY, part, LANES)
            landing = out.at[pl.ds(mine, GY), pl.ds(yh * part, part), :]
            if t < half - 1:
                goals = [2 * yp, 2 * yp + 1]
            else:
                goals = [yh + 1 - 2 * lax.rem(yh, 2)]

                @pl.when(core == k)
                def _():
                    pltpu.make_async_copy(back[k].at[yh], landing, l_out).start()

                @pl.when(core != k)
                def _():
                    remote(back[k].at[yh], landing, s_out, r_out, partner).start()

            for q in goals:
                remote(back[k].at[q], landing, s_out, r_out, (elem, q * 2 + k)).start()

    most = out.at[:, pl.ds(0, nb - part // 2), :]
    wait(back[0].at[0], l_out)
    wait(most, r_out)
    wait(most, s_out)
    for j in range(4):
        wait(own[0][0], s_init.at[j])
    for st in range(1, 6):
        for k in range(2):
            wait(own[st][k], s_far.at[st, k])
            wait(own[st][k], s_near.at[st, k])

    @pl.when(end_plane)
    def _():
        wait(rot.at[core, x, y, pl.ds(0, Z - 2)], s_z)

    @pl.when(inner_plane)
    def _():
        wait(rot.at[core, x, y, pl.ds(0, Z - 3)], s_z)
        wait(rot.at[core, x, pl.ds(0, Y - 1)], s_y)

    for n, plane in enumerate((1, Z - 2)):

        @pl.when(z == plane)
        def _():
            wait(slab, s_slab.at[n])

    wait(rot.at[core, pl.ds(0, X - 1)], s_x)
    wait(rot.at[core], s_core)
    for k in range(2):
        wait(gath[k].at[pl.ds(0, YH - 1)], s_a2a.at[k])


def build(mesh, X, YL, Z, YH):
    Y = YH * YL

    def body(start, blocks, neighbours, band_order, rotation):
        nb = start.shape[1]
        bands = band_order.shape[0]
        rows = rotation.shape[0]
        part = nb // YH
        kts = YH
        bf16 = jnp.bfloat16
        column = pltpu.VMEM((GY, nb, LANES), bf16)
        dma = pltpu.SemaphoreType.DMA
        hbm = pl.BlockSpec(memory_space=pl.ANY)
        return pl.pallas_call(
            functools.partial(kernel, X, YL, Z, YH),
            out_shape=jax.ShapeDtypeStruct(start.shape, bf16),
            in_specs=[hbm] * 5,
            out_specs=hbm,
            scratch_shapes=[
                pltpu.VMEM((GY, 5, nb, nb), bf16),
                pltpu.VMEM((kts, X, 2 * LANES, bands // X), bf16),
                pltpu.VMEM((2, X, Y, Z, rows, LANES), bf16),
                pltpu.VMEM((X, GY * part, bands // X), jnp.float32),
                pltpu.VMEM((X, GY * part, bands // X), bf16),
                pltpu.SMEM(neighbours.shape, jnp.int32),
                pltpu.SMEM((3, 6 * GY), jnp.int32),
                pltpu.VMEM((bands // LANES, LANES), jnp.int32),
                *[column] * 36,
                *[pltpu.VMEM((GY, nb, LANES), jnp.float32)] * 2,
                *[column] * 2,
                *[pltpu.VMEM((YH, GY, part, LANES), bf16)] * 4,
                *[dma((GY,)), dma((2,)), dma((4,)), dma((2,))],
                *[dma((6, 2)), dma((6, 2)), dma((6, 2)), dma((6, 2, GY))],
                *[dma, dma, dma, dma, dma, dma((2,)), dma, dma, dma((X - 1,)), dma, dma((X,))],
                *[dma((2,)), dma((2,)), dma((2,)), dma, dma, dma],
            ],
            compiler_params=pltpu.CompilerParams(collective_id=0, has_side_effects=True),
        )(start, blocks, neighbours, band_order.reshape(bands // LANES, LANES), rotation)

    return jax.shard_map(
        body,
        mesh=mesh,
        in_specs=(
            P("elem", None, "band"),
            P("elem", None, None, None),
            P("elem", None),
            P(),
            P("elem", "band"),
        ),
        out_specs=P("elem", None, "band"),
        check_vma=False,
    )


def solution(mesh):
    return build(mesh, **SIZES)
```

time: 341 us -> 76.8 us (0.23)
  blocking collectives: 152 us -> 0 us
  starting transfers between devices: 106 us -> 0 us
  Pallas kernels: 0 us -> 74.9 us
  waiting for transfers between devices: 23.9 us -> 0 us
  matrix products: 22.9 us -> 0 us
  local copies, waits for them, and re-layouts: 19.3 us -> 1.77 us
  between operations: 13.7 us -> 0.01 us
    all_gather x1 -> x0, blocking collectives: 136 us -> none  [body(): rotation_cols = lax.all_gather(rotation, 'elem', axis=0, tiled=True)]
    pallas_call x0 -> x1, Pallas kernels: none -> 74.9 us  [body(): pl.pallas_call(functools.partial(kernel, X, YL, Z, YH), out_shape=jax.Sha...]
    ppermute x12 -> x0, starting transfers between devices: 67.3 us -> none  [the longest x6 52.8 us: extended_2(): lax.ppermute(head, axis, [((i + 1) % count, i) for i in range(count)])]
    all_to_all x1 -> x0, starting transfers between devices: 38.3 us -> none  [body(): lax.all_to_all(flat_rows, 'band', split_axis=0, concat_axis=1, tiled=True)]
    dot_general x7 -> x0, matrix products: 22.9 us -> none  [the longest x6 22.4 us: apply_blocks(): jnp.einsum('esij,esjm->eim', blocks, picked, preferred_element_type=jnp.f...]
    ppermute x12 -> x0, waiting for transfers between devices: 18.2 us -> none  [the longest x6 12.1 us: extended_2(): lax.ppermute(head, axis, [((i + 1) % count, i) for i in range(count)])]
    all_to_all x1 -> x0, blocking collectives: 15.1 us -> none  [body(): lax.all_to_all(mixed_rows, 'band', split_axis=1, concat_axis=0, tiled=True)]
    gather x8 -> x0, local copies, waits for them, and re-layouts: 9.16 us -> none  [apply_blocks(): picked = jnp.take(extended, local_links, axis=0)]
  transfers between devices with their start and end apart: 14 -> 0, of which waited for: 11 -> 0; matrix products, arithmetic and copies ran while one was open for 8% -> 0% of each run, Pallas kernels for 0% -> 0%
where the time goes in v2:
time: 76.8 us; the launch traced here: 76.7 us
  Pallas kernels  74.9 us (98%)
  local copies, waits for them, and re-layouts  1.77 us (2%)
    pallas_call x1, Pallas kernels, body(): pl.pallas_call(functools.partial(kernel, X, YL, Z, YH), out_shape=jax.Sha...  74.9 us
    unnamed x1, local copies, waits for them, and re-layouts  1.77 us

profile of v2, /device:TPU:1, one launch (start us, length us, event | category | flops | bytes accessed | tf_op | source)
XLA Modules:
  0.0 76.7 jit_solution(6742814978299831947)
XLA Ops:
  0.0 74.9 %shard_map.55 = bf16[6,256,128]{2,1,0:T(8,128)(2,1)} custom-call(bf16[6,256,128]{2,1,0:T(8,128)(2,1)} %start.1, bf16[6,5,256,256]{3,2,1,0:T(8,128)(2,1)} %blocks.1, s32[6,5]{1,0:T(8,128)} %links_in.1, s32[8,128]{1,0:T(8,128)} %bitcast.1, bf16[16,128]{1,0:T(8,128)(2,1)} %rotation.1), custom_call_target="tpu_custom_call" | custom-call | tf_op jit(solution)/shard_map/pallas_call | solution.py:397
  74.9 1.8 %copy.7 = bf16[6,256,128]{2,1,0:T(8,128)(2,1)} copy(bf16[6,256,128]{2,1,0:T(8,128)(2,1)} %shard_map.55) | data formatting | bytes 786432

commit v3 on v2

--- a/solution.py
+++ b/solution.py
@@ -13,7 +13,7 @@
 SIZES = dict(X=4, YL=2, Z=8, YH=4)
 
 
-def kernel(X, YL, Z, YH, start, blocks, links_in, order_in, rotation, out, blk, perm, rot, racc, turned, links, table, order, *rest):
+def kernel(X, YL, Z, YH, start, blocks, links_in, order_in, rotation, out, blk, perm, rot, racc, turned, first, links, table, order, *rest):
     bf16, f32 = jnp.bfloat16, jnp.float32
     rest = list(rest)
 
@@ -85,6 +85,36 @@
 
     for i in range(GY):
         pltpu.make_async_copy(blocks.at[mine + i], blk.at[i], s_blk.at[i]).start()
+    wait(links, s_small.at[0])
+    t_near, t_far = 2 - core, 1 + core
+
+    def place(row, t):
+        return lax.rem(links[row, t], GY)
+
+    def slot_of(c, e):
+        return jnp.where(c == 1, place(GY + e, 2), e)
+
+    for j in range(GY):
+        second = jnp.where(place(GY, 2) == j, 0, jnp.where(place(GY + 1, 2) == j, 1, 2))
+        e = jnp.where(core == 0, j, second)
+        row = mine + e
+        ids = (place(row, 3), place(row, 4), place(row, t_near))
+        slots = (slot_of(core, ids[0]), slot_of(core, ids[1]), slot_of(1 - core, ids[2]))
+        for v, line in ((0, (e, e, *ids)), (1, (e, j, *slots))):
+            for n, value in enumerate(line):
+                table[v, j * 5 + n] = value
+        table[2, j] = slot_of(core, j)
+        table[2, GY + j] = second
+
+    for k, column in ((0, near[0][0]), (1, own[0][1])):
+
+        @pl.when(core == k)
+        def _():
+            wait(own[0][k], r_own.at[k])
+            wait(near[0][k], r_near.at[0, k])
+            for j in range(GY):
+                first[j] = column[table[2, GY + j]]
+
     pl.semaphore_wait(barrier, len(greeted))
 
     def at_end(c):
@@ -104,43 +134,21 @@
             remote(rotation, rot.at[core, x, y, z], s_z, r_z, dev).start()
 
     def first_far(k):
-        remote(start.at[pl.ds(mine, GY)], far[0][k], s_init.at[0], r_far.at[0, k, 0], zpeer).start()
-        remote(start.at[pl.ds(theirs, GY)], far[0][k], s_init.at[1], r_far.at[0, k, 0], zother).start()
+        for j in range(GY):
+            here = start.at[j]
+            for n, (src, dev) in enumerate(((first.at[j] if k else here, zpeer), (here if k else first.at[j], zother))):
+                remote(src, far[0][k].at[j], s_init.at[n], r_far.at[0, k, j], dev).start()
 
     for k in range(2):
 
         @pl.when(core == k)
         def _():
-            first_far(k)
+            if k == 0:
+                first_far(k)
             remote(start.at[pl.ds(theirs, GY)], own[0][k], s_init.at[2], r_own.at[k], partner).start()
             remote(start.at[pl.ds(mine, GY)], near[0][k], s_init.at[3], r_near.at[0, k], partner).start()
 
-    wait(links, s_small.at[0])
     wait(order, s_small.at[1])
-    t_near, t_far = 2 - core, 1 + core
-
-    def place(row, t):
-        return lax.rem(links[row, t], GY)
-
-    def slot_of(c, e):
-        return jnp.where(c == 1, place(GY + e, 2), e)
-
-    for j in range(GY):
-        e = jnp.where(
-            core == 0,
-            j,
-            jnp.where(place(GY, 2) == j, 0, jnp.where(place(GY + 1, 2) == j, 1, 2)),
-        )
-        for v, at in ((0, e), (1, e), (2, j)):
-            row = mine + at
-            ids = (place(row, 3), place(row, 4), place(row, t_near), place(row, t_far))
-            if v == 0:
-                line = (at, at, *ids)
-            else:
-                here = j if v == 1 else slot_of(core, at)
-                line = (at, here, slot_of(core, ids[0]), slot_of(core, ids[1]), slot_of(1 - core, ids[2]), here)
-            for n, value in enumerate(line):
-                table[v, j * 6 + n] = value
 
     kts, width = perm.shape[0], perm.shape[3]
 
@@ -156,16 +164,16 @@
         return carry
 
     def row_of(st):
-        return 0 if st == 0 else 2 if st == 5 else 1
+        return 0 if st == 0 else 1
 
     def before(st, k):
         v = row_of(st)
 
         def one(j, carry):
-            e = table[v, j * 6]
-            total = jnp.dot(blk[e, t_near], near[st][k][table[v, j * 6 + 4]], preferred_element_type=f32)
+            e = table[v, j * 5]
+            total = jnp.dot(blk[e, t_near], near[st][k][table[v, j * 5 + 4]], preferred_element_type=f32)
             for n, t in ((1, 0), (2, 3), (3, 4)):
-                total += jnp.dot(blk[e, t], own[st][k][table[v, j * 6 + n]], preferred_element_type=f32)
+                total += jnp.dot(blk[e, t], own[st][k][table[v, j * 5 + n]], preferred_element_type=f32)
             acc[k][j] = total
             return carry
 
@@ -186,22 +194,12 @@
 
     def after(st, k):
         v = row_of(st)
-        if st == 0:
-            wait(far[0][k], r_far.at[0, k, 0])
-        if st == 5:
-            for j in range(GY):
-                wait(far[st][k].at[j], r_far.at[st, k, j])
-
         def one(j, carry):
-            e = table[v, j * 6]
-            if st in (0, 5):
-                there = far[st][k][table[v, j * 6 + 5]]
-            else:
-                wait(far[st][k].at[j], r_far.at[st, k, j])
-                there = far[st][k][j]
-            total = acc[k][j] + jnp.dot(blk[e, t_far], there, preferred_element_type=f32)
+            e = table[v, j * 5]
+            wait(far[st][k].at[j], r_far.at[st, k, j])
+            total = acc[k][j] + jnp.dot(blk[e, t_far], far[st][k][j], preferred_element_type=f32)
             if st % 3:
-                previous = own[st - 1][k][e if st == 1 else table[v, j * 6 + 1]]
+                previous = own[st - 1][k][e if st == 1 else j]
                 total = 2.0 * total - previous.astype(f32)
             if st < 5:
                 own[st + 1][k][j] = total.astype(bf16)
@@ -218,14 +216,23 @@
         before(st, k)
 
     lax.fori_loop(0, kts * X, one_hot, 0)
-    wait(own[0][0], r_own.at[0])
-    wait(near[0][0], r_near.at[0, 0])
+
+    @pl.when(core == 1)
+    def _():
+        wait(own[0][0], r_own.at[0])
+        wait(near[0][0], r_near.at[0, 0])
+        first_far(1)
 
     for i in range(GY):
         wait(blk.at[i], s_blk.at[i])
     before(0, 0)
-    wait(own[0][1], r_own.at[1])
-    early(0, 1)
+
+    @pl.when(core == 0)
+    def _():
+        wait(own[0][1], r_own.at[1])
+        wait(near[0][1], r_near.at[0, 1])
+
+    before(0, 1)
 
     slab = rot.at[core, x]
 
@@ -236,14 +243,28 @@
         for d in range(1, Y):
             remote(at, at, s_y, r_y, y_peers[d - 1]).start()
 
-    def along_x():
-        for d in range(1, X):
-            remote(slab, slab, s_x, r_x.at[d - 1], x_peers[d - 1]).start()
+    beside = [d for d in range(1, X) if d in (1, X - 1)]
+    others = [d for d in range(1, X) if d not in beside]
+
+    def to_end_plane(at, n, sem):
+        for m, (plane, step) in enumerate(((1, -1), (Z - 2, 1))):
+
+            @pl.when(z == plane)
+            def _():
+                remote(at, at, s_slab.at[n, m], sem, (elem + step, band)).start()
+
+    def inner_spread():
+        wait(rot.at[core, x, pl.ds(0, Y - 1)], r_y)
+        to_end_plane(slab, 0, r_slab)
+        for d in others + beside:
+            remote(slab, slab, s_x.at[d - 1], r_x.at[d - 1], x_peers[d - 1]).start()
         remote(slab, slab, s_core, r_core.at[0], partner).start()
 
-    pieces = [(yy, d) for yy in range(Y) for d in range(1, X)]
-
-    def along_x_in_turn(turn, turns):
+    pieces = [(yy, d) for yy in range(Y) for d in beside]
+
+    def along_x_in_turn(turn):
+        turns = 6
+
         @pl.when(end_plane)
         def _():
             if turn == 0:
@@ -251,56 +272,47 @@
                 remote(slab, slab, s_core, r_core.at[0], partner).start()
             for yy, d in pieces[turn * len(pieces) // turns : (turn + 1) * len(pieces) // turns]:
                 at = rot.at[core, x, yy]
-                remote(at, at, s_x, r_x.at[d - 1], x_peers[d - 1]).start()
-
-    def hand_over():
-        for d in range(1, X):
+                remote(at, at, s_x.at[d - 1], r_x.at[d - 1], x_peers[d - 1]).start()
+
+    def hand_over(ds):
+        for d in ds:
             at = rot.at[core, lax.rem(x - d + X, X)]
             wait(at, r_x.at[d - 1])
             remote(at, at, s_core, r_core.at[d], partner).start()
+            if d in others:
+                to_end_plane(at, d, r_x.at[d - 1])
 
     for st in range(6):
+        if st == 5:
+            pl.when(inner_plane)(lambda: hand_over(others))
         after(st, 0)
-        if st == 0:
+        if st == 1:
             pl.when(inner_plane)(along_y)
-        if st == 1:
-
-            @pl.when(inner_plane)
-            def _():
-                wait(rot.at[core, x, pl.ds(0, Y - 1)], r_y)
-
-                @pl.when(z == 1)
-                def _():
-                    remote(slab, slab, s_slab.at[0], r_slab, (elem - 1, band)).start()
-
-                @pl.when(z == Z - 2)
-                def _():
-                    remote(slab, slab, s_slab.at[1], r_slab, (elem + 1, band)).start()
-
-                along_x()
-
-        turn = 4 * (st - 2)
-        if 2 <= st < 5:
-            along_x_in_turn(turn, 12)
-        if st == 4:
-            pl.when(inner_plane)(hand_over)
+        if st == 3:
+            pl.when(inner_plane)(inner_spread)
+        if st > 3:
+            along_x_in_turn(4 * (st - 4))
         if st:
             early(st, 1)
-        if 2 <= st < 5:
-            along_x_in_turn(turn + 1, 12)
+        if st > 3:
+            along_x_in_turn(4 * (st - 4) + 1)
         after(st, 1)
-        if 2 <= st < 5:
-            along_x_in_turn(turn + 2, 12)
+        if st == 4:
+            along_x_in_turn(2)
         if st < 5:
             early(st + 1, 0)
-        if 2 <= st < 5:
-            along_x_in_turn(turn + 3, 12)
-    pl.when(end_plane)(hand_over)
+        if st == 4:
+            along_x_in_turn(3)
+    hand_over(beside)
+    pl.when(end_plane)(lambda: hand_over(others))
+
+    def rows_of(k, q):
+        return jnp.concatenate([gath[k][q, table[2, i]] for i in range(GY)], axis=0)
 
     def reordered(k, xx):
         total = None
         for yp in range(half):
-            sides = [gath[k][2 * yp + h].reshape(GY * part, LANES) for h in range(2)]
+            sides = [rows_of(k, 2 * yp + h) for h in range(2)]
             term = jnp.dot(jnp.concatenate(sides, axis=1), perm[k * half + yp, xx], preferred_element_type=f32)
             total = term if total is None else total + term
         return total
@@ -369,13 +381,21 @@
         wait(rot.at[core, x, y, pl.ds(0, Z - 3)], s_z)
         wait(rot.at[core, x, pl.ds(0, Y - 1)], s_y)
 
-    for n, plane in enumerate((1, Z - 2)):
+    for m, plane in enumerate((1, Z - 2)):
 
         @pl.when(z == plane)
         def _():
-            wait(slab, s_slab.at[n])
-
-    wait(rot.at[core, pl.ds(0, X - 1)], s_x)
+            for n in (0, *others):
+                wait(slab, s_slab.at[n, m])
+
+    for d in beside:
+        wait(slab, s_x.at[d - 1])
+
+    @pl.when(inner_plane)
+    def _():
+        for d in others:
+            wait(slab, s_x.at[d - 1])
+
     wait(rot.at[core], s_core)
     for k in range(2):
         wait(gath[k].at[pl.ds(0, YH - 1)], s_a2a.at[k])
@@ -396,7 +416,7 @@
         hbm = pl.BlockSpec(memory_space=pl.ANY)
         return pl.pallas_call(
             functools.partial(kernel, X, YL, Z, YH),
-            out_shape=jax.ShapeDtypeStruct(start.shape, bf16),
+            out_shape=pltpu.VMEM(start.shape, bf16),
             in_specs=[hbm] * 5,
             out_specs=hbm,
             scratch_shapes=[
@@ -405,6 +425,7 @@
                 pltpu.VMEM((2, X, Y, Z, rows, LANES), bf16),
                 pltpu.VMEM((X, GY * part, bands // X), jnp.float32),
                 pltpu.VMEM((X, GY * part, bands // X), bf16),
+                column,
                 pltpu.SMEM(neighbours.shape, jnp.int32),
                 pltpu.SMEM((3, 6 * GY), jnp.int32),
                 pltpu.VMEM((bands // LANES, LANES), jnp.int32),
@@ -414,7 +435,7 @@
                 *[pltpu.VMEM((YH, GY, part, LANES), bf16)] * 4,
                 *[dma((GY,)), dma((2,)), dma((4,)), dma((2,))],
                 *[dma((6, 2)), dma((6, 2)), dma((6, 2)), dma((6, 2, GY))],
-                *[dma, dma, dma, dma, dma, dma((2,)), dma, dma, dma((X - 1,)), dma, dma((X,))],
+                *[dma, dma, dma, dma, dma, dma((X, 2)), dma, dma((X - 1,)), dma((X - 1,)), dma, dma((X,))],
                 *[dma((2,)), dma((2,)), dma((2,)), dma, dma, dma],
             ],
             compiler_params=pltpu.CompilerParams(collective_id=0, has_side_effects=True),

time: 76.8 us -> 72.6 us (0.945)
  Pallas kernels: 74.9 us -> 71.4 us
  local copies, waits for them, and re-layouts: 1.77 us -> 0.75 us
    pallas_call x1, Pallas kernels: 74.9 us -> 71.4 us  [body(): pl.pallas_call(functools.partial(kernel, X, YL, Z, YH), out_shape=pltpu.V...]
    unnamed x1, local copies, waits for them, and re-layouts: 1.77 us -> 0.75 us
where the time goes in v3:
time: 72.6 us; the launch traced here: 72.2 us
  Pallas kernels  71.4 us (98%)
  local copies, waits for them, and re-layouts  0.75 us (1%)
    pallas_call x1, Pallas kernels, body(): pl.pallas_call(functools.partial(kernel, X, YL, Z, YH), out_shape=pltpu.V...  71.4 us

profile of v3, /device:TPU:1, one launch (start us, length us, event | category | flops | bytes accessed | tf_op | source)
XLA Modules:
  0.0 72.2 jit_solution(13999411338621956217)
XLA Ops:
  0.0 71.4 %shard_map.55 = bf16[6,256,128]{2,1,0:T(8,128)(2,1)S(1)} custom-call(bf16[6,256,128]{2,1,0:T(8,128)(2,1)} %start.1, bf16[6,5,256,256]{3,2,1,0:T(8,128)(2,1)} %blocks.1, s32[6,5]{1,0:T(8,128)} %links_in.1, s32[8,128]{1,0:T(8,128)} %bitcast.1, bf16[16,128]{1,0:T(8,128)(2,1)} %rotation.1), custom_call_target="tpu_custom_call" | custom-call | tf_op jit(solution)/shard_map/pallas_call | solution.py:417
  71.4 0.7 %copy.7 = bf16[6,256,128]{2,1,0:T(8,128)(2,1)} copy(bf16[6,256,128]{2,1,0:T(8,128)(2,1)S(1)} %shard_map.55) | data formatting | bytes 786432

commit v4 on v3

--- a/solution.py
+++ b/solution.py
@@ -28,6 +28,7 @@
     filt = take(2)
     gath = take(2)
     back = take(2)
+    (landed,) = take(1)
     (
         (s_blk, s_small, s_init, r_own, s_near, r_near, s_far, r_far),
         (s_z, r_z, l_rot, s_y, r_y, s_slab, r_slab, s_x, r_x, s_core, r_core),
@@ -92,7 +93,7 @@
         return lax.rem(links[row, t], GY)
 
     def slot_of(c, e):
-        return jnp.where(c == 1, place(GY + e, 2), e)
+        return e if isinstance(c, int) and c == 0 else jnp.where(c == 1, place(GY + e, 2), e)
 
     for j in range(GY):
         second = jnp.where(place(GY, 2) == j, 0, jnp.where(place(GY + 1, 2) == j, 1, 2))
@@ -103,8 +104,7 @@
         for v, line in ((0, (e, e, *ids)), (1, (e, j, *slots))):
             for n, value in enumerate(line):
                 table[v, j * 5 + n] = value
-        table[2, j] = slot_of(core, j)
-        table[2, GY + j] = second
+        table[2, j] = second
 
     for k, column in ((0, near[0][0]), (1, own[0][1])):
 
@@ -113,7 +113,7 @@
             wait(own[0][k], r_own.at[k])
             wait(near[0][k], r_near.at[0, k])
             for j in range(GY):
-                first[j] = column[table[2, GY + j]]
+                first[j] = column[table[2, j]]
 
     pl.semaphore_wait(barrier, len(greeted))
 
@@ -126,12 +126,6 @@
     @pl.when(inner_plane)
     def _():
         pltpu.make_async_copy(rotation, rot.at[core, x, y, z], l_rot).start()
-
-    for d, dev in enumerate(z_peers):
-
-        @pl.when(jnp.logical_not(at_end(lax.rem(z + d + 1, Z))))
-        def _():
-            remote(rotation, rot.at[core, x, y, z], s_z, r_z, dev).start()
 
     def first_far(k):
         for j in range(GY):
@@ -147,6 +141,12 @@
                 first_far(k)
             remote(start.at[pl.ds(theirs, GY)], own[0][k], s_init.at[2], r_own.at[k], partner).start()
             remote(start.at[pl.ds(mine, GY)], near[0][k], s_init.at[3], r_near.at[0, k], partner).start()
+
+    for d, dev in enumerate(z_peers):
+
+        @pl.when(jnp.logical_not(at_end(lax.rem(z + d + 1, Z))))
+        def _():
+            remote(rotation, rot.at[core, x, y, z], s_z, r_z, dev).start()
 
     wait(order, s_small.at[1])
 
@@ -188,9 +188,9 @@
         for d in range(1, YH):
             q = lax.rem(yh + d, YH)
             src = filt[k].at[j, pl.ds(q * part, part)]
-            remote(src, gath[k].at[yh, j], s_a2a.at[k], r_a2a.at[k], a_peers[d - 1]).start()
+            remote(src, gath[k].at[j, yh], s_a2a.at[k], r_a2a.at[k, j], a_peers[d - 1]).start()
         src = filt[k].at[j, pl.ds(yh * part, part)]
-        pltpu.make_async_copy(src, gath[k].at[yh, j], l_a2a.at[k]).start()
+        pltpu.make_async_copy(src, gath[k].at[j, yh], l_a2a.at[k, j]).start()
 
     def after(st, k):
         v = row_of(st)
@@ -260,19 +260,11 @@
             remote(slab, slab, s_x.at[d - 1], r_x.at[d - 1], x_peers[d - 1]).start()
         remote(slab, slab, s_core, r_core.at[0], partner).start()
 
-    pieces = [(yy, d) for yy in range(Y) for d in beside]
-
-    def along_x_in_turn(turn):
-        turns = 6
-
-        @pl.when(end_plane)
-        def _():
-            if turn == 0:
-                wait(slab, r_slab)
-                remote(slab, slab, s_core, r_core.at[0], partner).start()
-            for yy, d in pieces[turn * len(pieces) // turns : (turn + 1) * len(pieces) // turns]:
-                at = rot.at[core, x, yy]
-                remote(at, at, s_x.at[d - 1], r_x.at[d - 1], x_peers[d - 1]).start()
+    def end_spread():
+        wait(slab, r_slab)
+        for d in beside:
+            remote(slab, slab, s_x.at[d - 1], r_x.at[d - 1], x_peers[d - 1]).start()
+        remote(slab, slab, s_core, r_core.at[0], partner).start()
 
     def hand_over(ds):
         for d in ds:
@@ -290,81 +282,77 @@
             pl.when(inner_plane)(along_y)
         if st == 3:
             pl.when(inner_plane)(inner_spread)
-        if st > 3:
-            along_x_in_turn(4 * (st - 4))
         if st:
             early(st, 1)
-        if st > 3:
-            along_x_in_turn(4 * (st - 4) + 1)
         after(st, 1)
         if st == 4:
-            along_x_in_turn(2)
+            pl.when(end_plane)(end_spread)
         if st < 5:
             early(st + 1, 0)
-        if st == 4:
-            along_x_in_turn(3)
-    hand_over(beside)
-    pl.when(end_plane)(lambda: hand_over(others))
-
-    def rows_of(k, q):
-        return jnp.concatenate([gath[k][q, table[2, i]] for i in range(GY)], axis=0)
-
-    def reordered(k, xx):
+    def reordered(k, j, xx):
         total = None
         for yp in range(half):
-            sides = [rows_of(k, 2 * yp + h) for h in range(2)]
-            term = jnp.dot(jnp.concatenate(sides, axis=1), perm[k * half + yp, xx], preferred_element_type=f32)
+            both = jnp.concatenate([gath[k][j, 2 * yp + h] for h in range(2)], axis=1)
+            term = jnp.dot(both, perm[k * half + yp, xx], preferred_element_type=f32)
             total = term if total is None else total + term
         return total
 
-    def first_half(xx, carry):
-        racc[xx] = reordered(0, xx)
+    def arrived(k, j):
+        wait(gath[k].at[j, 0], l_a2a.at[k, j])
+        wait(gath[k].at[j, pl.ds(0, YH - 1)], r_a2a.at[k, j])
+
+    def first_half(j, carry):
+        arrived(0, j)
+        for xx in range(X):
+            racc[j, xx] = reordered(0, j, xx)
         return carry
 
-    def second_half(xx, carry):
-        turned[xx] = (racc[xx] + reordered(1, xx)).astype(bf16)
-        return carry
-
-    for k in range(2):
-        wait(gath[k].at[0], l_a2a.at[k])
-        wait(gath[k].at[pl.ds(0, YH - 1)], r_a2a.at[k])
-        if k == 0:
-            lax.fori_loop(0, X, first_half, 0)
-    lax.fori_loop(0, X, second_half, 0)
-    for d in range(X):
-        wait(rot.at[core, 0], r_core.at[d])
-    for k in range(2):
+    def second_half(j):
+        arrived(1, j)
+        for xx in range(X):
+            turned[j, xx] = (racc[j, xx] + reordered(1, j, xx)).astype(bf16)
+
+    def rotate(j, m):
+        goal = core if m == 0 else 1 - core
+        landing = landed.at[mine + j, pl.ds(yh * part, part), :]
         for t in range(half):
             yp = lax.rem(lax.div(yh, 2) + 1 + t, half)
             total = None
             for xx in range(X):
-                sides = [rot[k, xx, pl.ds((2 * yp + h) * YL, YL)].reshape(width, LANES) for h in range(2)]
-                term = jnp.dot(turned[xx], jnp.concatenate(sides, axis=1), preferred_element_type=f32)
+                both = [rot[goal, xx, pl.ds((2 * yp + h) * YL, YL)].reshape(width, LANES) for h in range(2)]
+                term = jnp.dot(turned[j, xx], jnp.concatenate(both, axis=1), preferred_element_type=f32)
                 total = term if total is None else total + term
             total = total.astype(bf16)
             for h in range(2):
-                back[k][2 * yp + h] = total[:, h * LANES : (h + 1) * LANES].reshape(GY, part, LANES)
-            landing = out.at[pl.ds(mine, GY), pl.ds(yh * part, part), :]
+                back[m][j, 2 * yp + h] = total[:, h * LANES : (h + 1) * LANES]
             if t < half - 1:
                 goals = [2 * yp, 2 * yp + 1]
             else:
                 goals = [yh + 1 - 2 * lax.rem(yh, 2)]
-
-                @pl.when(core == k)
-                def _():
-                    pltpu.make_async_copy(back[k].at[yh], landing, l_out).start()
-
-                @pl.when(core != k)
-                def _():
-                    remote(back[k].at[yh], landing, s_out, r_out, partner).start()
-
+                if m == 0:
+                    pltpu.make_async_copy(back[m].at[j, yh], landing, l_out).start()
+                else:
+                    goals = [*goals, yh]
             for q in goals:
-                remote(back[k].at[q], landing, s_out, r_out, (elem, q * 2 + k)).start()
-
-    most = out.at[:, pl.ds(0, nb - part // 2), :]
-    wait(back[0].at[0], l_out)
-    wait(most, r_out)
-    wait(most, s_out)
+                remote(back[m].at[j, q], landing, s_out, r_out, (elem, q * 2 + goal)).start()
+
+    def own_bands(j, carry):
+        second_half(j)
+        rotate(j, 0)
+        return carry
+
+    def other_bands(j, carry):
+        rotate(j, 1)
+        return carry
+
+    lax.fori_loop(0, GY, first_half, 0)
+    hand_over(beside)
+    pl.when(end_plane)(lambda: hand_over(others))
+    lax.fori_loop(0, GY, own_bands, 0)
+    for d in range(X):
+        wait(rot.at[core, 0], r_core.at[d])
+    lax.fori_loop(0, GY, other_bands, 0)
+
     for j in range(4):
         wait(own[0][0], s_init.at[j])
     for st in range(1, 6):
@@ -398,7 +386,14 @@
 
     wait(rot.at[core], s_core)
     for k in range(2):
-        wait(gath[k].at[pl.ds(0, YH - 1)], s_a2a.at[k])
+        wait(gath[k].at[:, pl.ds(0, YH - 1)], s_a2a.at[k])
+    most = landed.at[:, pl.ds(0, nb - part // 2), :]
+    wait(landed.at[pl.ds(0, GY), pl.ds(0, part), :], l_out)
+    wait(most, s_out)
+    wait(most, r_out)
+    for c in range(2):
+        for i in range(GY):
+            out[c * GY + i] = landed[c * GY + slot_of(c, i)]
 
 
 def build(mesh, X, YL, Z, YH):
@@ -418,13 +413,13 @@
             functools.partial(kernel, X, YL, Z, YH),
             out_shape=pltpu.VMEM(start.shape, bf16),
             in_specs=[hbm] * 5,
-            out_specs=hbm,
+            out_specs=pl.BlockSpec(memory_space=pltpu.VMEM),
             scratch_shapes=[
                 pltpu.VMEM((GY, 5, nb, nb), bf16),
                 pltpu.VMEM((kts, X, 2 * LANES, bands // X), bf16),
                 pltpu.VMEM((2, X, Y, Z, rows, LANES), bf16),
-                pltpu.VMEM((X, GY * part, bands // X), jnp.float32),
-                pltpu.VMEM((X, GY * part, bands // X), bf16),
+                pltpu.VMEM((GY, X, part, bands // X), jnp.float32),
+                pltpu.VMEM((GY, X, part, bands // X), bf16),
                 column,
                 pltpu.SMEM(neighbours.shape, jnp.int32),
                 pltpu.SMEM((3, 6 * GY), jnp.int32),
@@ -432,11 +427,12 @@
                 *[column] * 36,
                 *[pltpu.VMEM((GY, nb, LANES), jnp.float32)] * 2,
                 *[column] * 2,
-                *[pltpu.VMEM((YH, GY, part, LANES), bf16)] * 4,
+                *[pltpu.VMEM((GY, YH, part, LANES), bf16)] * 4,
+                pltpu.VMEM(start.shape, bf16),
                 *[dma((GY,)), dma((2,)), dma((4,)), dma((2,))],
                 *[dma((6, 2)), dma((6, 2)), dma((6, 2)), dma((6, 2, GY))],
                 *[dma, dma, dma, dma, dma, dma((X, 2)), dma, dma((X - 1,)), dma((X - 1,)), dma, dma((X,))],
-                *[dma((2,)), dma((2,)), dma((2,)), dma, dma, dma],
+                *[dma((2,)), dma((2, GY)), dma((2, GY)), dma, dma, dma],
             ],
             compiler_params=pltpu.CompilerParams(collective_id=0, has_side_effects=True),
         )(start, blocks, neighbours, band_order.reshape(bands // LANES, LANES), rotation)

time: 72.6 us -> 70.6 us (0.972)
  Pallas kernels: 71.4 us -> 69.7 us
    pallas_call x1, Pallas kernels: 71.4 us -> 69.7 us  [body(): pl.pallas_call(functools.partial(kernel, X, YL, Z, YH), out_shape=pltpu.V...]
where the time goes in v4:
time: 70.6 us; the launch traced here: 70.5 us
  Pallas kernels  69.7 us (99%)
  local copies, waits for them, and re-layouts  0.75 us (1%)
    pallas_call x1, Pallas kernels, body(): pl.pallas_call(functools.partial(kernel, X, YL, Z, YH), out_shape=pltpu.V...  69.7 us

profile of v4, /device:TPU:1, one launch (start us, length us, event | category | flops | bytes accessed | tf_op | source)
XLA Modules:
  0.0 70.5 jit_solution(13847467029601423891)
XLA Ops:
  0.0 69.7 %shard_map.55 = bf16[6,256,128]{2,1,0:T(8,128)(2,1)S(1)} custom-call(bf16[6,256,128]{2,1,0:T(8,128)(2,1)} %start.1, bf16[6,5,256,256]{3,2,1,0:T(8,128)(2,1)} %blocks.1, s32[6,5]{1,0:T(8,128)} %links_in.1, s32[8,128]{1,0:T(8,128)} %bitcast.1, bf16[16,128]{1,0:T(8,128)(2,1)} %rotation.1), custom_call_target="tpu_custom_call" | custom-call | tf_op jit(solution)/shard_map/pallas_call | solution.py:412
  69.8 0.7 %copy.7 = bf16[6,256,128]{2,1,0:T(8,128)(2,1)} copy(bf16[6,256,128]{2,1,0:T(8,128)(2,1)S(1)} %shard_map.55) | data formatting | bytes 786432

commit v5 on v4

--- a/solution.py
+++ b/solution.py
@@ -66,16 +66,15 @@
     x_peers = [((lax.rem(x + d, X) * YL + yl) * Z + z, band) for d in range(1, X)]
     a_peers = [(elem, lax.rem(yh + d, YH) * 2 + core) for d in range(1, YH)]
 
+    pltpu.make_async_copy(links_in, links, s_small.at[0]).start()
+
     barrier = pltpu.get_barrier_semaphore()
-    greeted = [partner] + z_peers + y_peers + x_peers
+    greeted = [(lax.rem(elem + step, E), yh * 2 + c) for c in range(2) for step in (1, E - 1)]
+    greeted += [partner] + z_peers + y_peers + x_peers
     greeted += [(elem, lax.rem(yh + d, YH) * 2 + 1 - core) for d in range(1, YH)]
-    for step in (1, E - 1):
-        for c in range(2):
-            greeted.append((lax.rem(elem + step, E), yh * 2 + c))
     for dev in greeted:
         pl.semaphore_signal(barrier, inc=1, device_id=dev, device_id_type=MESH)
 
-    pltpu.make_async_copy(links_in, links, s_small.at[0]).start()
     pltpu.make_async_copy(order_in, order, s_small.at[1]).start()
     for k in range(2):
 
@@ -185,7 +184,7 @@
         remote(src, near[st][k].at[j], s_near.at[st, k], r_near.at[st, k], partner).start()
 
     def exchange(k, j):
-        for d in range(1, YH):
+        for d in sorted(range(1, YH), key=lambda d: -min(d, YH - d)):
             q = lax.rem(yh + d, YH)
             src = filt[k].at[j, pl.ds(q * part, part)]
             remote(src, gath[k].at[j, yh], s_a2a.at[k], r_a2a.at[k, j], a_peers[d - 1]).start()
@@ -277,11 +276,11 @@
     for st in range(6):
         if st == 5:
             pl.when(inner_plane)(lambda: hand_over(others))
+        if st == 3:
+            pl.when(inner_plane)(inner_spread)
         after(st, 0)
         if st == 1:
             pl.when(inner_plane)(along_y)
-        if st == 3:
-            pl.when(inner_plane)(inner_spread)
         if st:
             early(st, 1)
         after(st, 1)

time: 70.6 us -> 70.5 us (level)
  no operation moved by 1% of the time
where the time goes in v5:
time: 70.5 us; the launch traced here: 70.4 us
  Pallas kernels  69.6 us (99%)
  local copies, waits for them, and re-layouts  0.75 us (1%)
    pallas_call x1, Pallas kernels, body(): pl.pallas_call(functools.partial(kernel, X, YL, Z, YH), out_shape=pltpu.V...  69.6 us

profile of v5, /device:TPU:1, one launch (start us, length us, event | category | flops | bytes accessed | tf_op | source)
XLA Modules:
  0.0 70.4 jit_solution(15998182953011457288)
XLA Ops:
  0.0 69.6 %shard_map.55 = bf16[6,256,128]{2,1,0:T(8,128)(2,1)S(1)} custom-call(bf16[6,256,128]{2,1,0:T(8,128)(2,1)} %start.1, bf16[6,5,256,256]{3,2,1,0:T(8,128)(2,1)} %blocks.1, s32[6,5]{1,0:T(8,128)} %links_in.1, s32[8,128]{1,0:T(8,128)} %bitcast.1, bf16[16,128]{1,0:T(8,128)(2,1)} %rotation.1), custom_call_target="tpu_custom_call" | custom-call | tf_op jit(solution)/shard_map/pallas_call | solution.py:411
  69.6 0.7 %copy.7 = bf16[6,256,128]{2,1,0:T(8,128)(2,1)} copy(bf16[6,256,128]{2,1,0:T(8,128)(2,1)S(1)} %shard_map.55) | data formatting | bytes 786432

commit v6 on v5

--- a/solution.py
+++ b/solution.py
@@ -273,9 +273,10 @@
             if d in others:
                 to_end_plane(at, d, r_x.at[d - 1])
 
+    beside_end = jnp.logical_or(z == 1, z == Z - 2)
     for st in range(6):
         if st == 5:
-            pl.when(inner_plane)(lambda: hand_over(others))
+            pl.when(jnp.logical_and(inner_plane, jnp.logical_not(beside_end)))(lambda: hand_over(others))
         if st == 3:
             pl.when(inner_plane)(inner_spread)
         after(st, 0)
@@ -285,9 +286,11 @@
             early(st, 1)
         after(st, 1)
         if st == 4:
-            pl.when(end_plane)(end_spread)
+            pl.when(beside_end)(lambda: hand_over(others))
         if st < 5:
             early(st + 1, 0)
+        if st == 4:
+            pl.when(end_plane)(end_spread)
     def reordered(k, j, xx):
         total = None
         for yp in range(half):

time: 70.5 us -> 70.6 us (level)
  no operation moved by 1% of the time
where the time goes in v6:
time: 70.6 us; the launch traced here: 70.5 us
  Pallas kernels  69.7 us (99%)
  local copies, waits for them, and re-layouts  0.75 us (1%)
    pallas_call x1, Pallas kernels, body(): pl.pallas_call(functools.partial(kernel, X, YL, Z, YH), out_shape=pltpu.V...  69.7 us

profile of v6, /device:TPU:1, one launch (start us, length us, event | category | flops | bytes accessed | tf_op | source)
XLA Modules:
  0.0 70.5 jit_solution(8670041339953476207)
XLA Ops:
  0.0 69.7 %shard_map.55 = bf16[6,256,128]{2,1,0:T(8,128)(2,1)S(1)} custom-call(bf16[6,256,128]{2,1,0:T(8,128)(2,1)} %start.1, bf16[6,5,256,256]{3,2,1,0:T(8,128)(2,1)} %blocks.1, s32[6,5]{1,0:T(8,128)} %links_in.1, s32[8,128]{1,0:T(8,128)} %bitcast.1, bf16[16,128]{1,0:T(8,128)(2,1)} %rotation.1), custom_call_target="tpu_custom_call" | custom-call | tf_op jit(solution)/shard_map/pallas_call | solution.py:414
  69.7 0.7 %copy.7 = bf16[6,256,128]{2,1,0:T(8,128)(2,1)} copy(bf16[6,256,128]{2,1,0:T(8,128)(2,1)S(1)} %shard_map.55) | data formatting | bytes 786432
